TPU v7x, 32 devices: a whole 2x2x4 slice. The times are simulated.
32 devices in a mesh: inp: 8 (over z, x), tm: 4 (over y, core).
Axes of the slice: x: 2, y: 2, z: 4, core: 2. Of those that a mesh axis runs over, the one named last changes fastest.
Arguments:
- samples: bfloat16 [576, 2, 24576], P('inp', None, 'tm'), may hold values from -6 to 6
- delays: int32 [576], P('inp'), may hold values from 0 to 3840
- taps: int32 [16, 256], replicated, may hold values from -2048 to 2047
Outputs:
- visibilities: float32 [256, 576, 1152], P('inp', 'tm')
All inputs are finite; a program needn't handle non-finite values.
Results may differ from a plain program's by a relative error of at most 0.0031.
Values may be sent and summed in bfloat16 or wider, within the bound.
A program may use at most 128 MiB of HBM per device.

v0:
```python
import math

import jax
import jax.numpy as jnp
from jax import lax
from jax.sharding import PartitionSpec as P


def with_halo(value, sides, width):
    for axis, dim in sides:
        peers, length = (lax.axis_size(axis), value.shape[dim])
        up = [(i, (i + 1) % peers) for i in range(peers)]
        down = [(j, i) for i, j in up]
        last = lax.slice_in_dim(value, length - width, length, axis=dim)
        leading = lax.slice_in_dim(value, 0, width, axis=dim)
        before = lax.ppermute(last, axis, up)
        after = lax.ppermute(leading, axis, down)
        value = jnp.concatenate([before, value, after], axis=dim)
    return value


def dft_table(length):
    channel_index = jnp.arange(length, dtype=jnp.int32)
    phase = (jnp.outer(channel_index, channel_index) % length).astype(jnp.float32) * (
        2.0 * math.pi / length
    )
    cosine = jnp.cos(phase)
    sine = jnp.sin(phase)
    upper = jnp.concatenate([cosine, -sine], axis=1)
    lower = jnp.concatenate([sine, cosine], axis=1)
    return jnp.concatenate([upper, lower], axis=0) / math.sqrt(length)


def shards(samples, delays, taps):
    tap_count, channels = taps.shape
    local_inputs, _, shard_len = samples.shape
    margin = (tap_count - 1) * channels
    local_spectra = shard_len // channels
    padded = with_halo(samples, (("tm", 2),), margin)
    window = shard_len + margin

    def align(series, offset):
        return lax.dynamic_slice_in_dim(series, offset, window, 1)

    aligned = jax.vmap(align)(padded, delays).astype(jnp.float32)
    frames = aligned.reshape(local_inputs, 2, local_spectra + tap_count - 1, channels)
    coefficient = taps.astype(jnp.float32) * (1.0 / 4096.0)
    filtered = jnp.zeros((local_inputs, 2, local_spectra, channels), jnp.float32)
    for tap in range(tap_count):
        begin = tap_count - 1 - tap
        filtered = (
            filtered
            + coefficient[tap][None, None, None, :] * frames[:, :, begin : begin + local_spectra, :]
        )
    table = dft_table(channels).reshape(2, channels, 2, channels)
    spectra = jnp.einsum(
        "icsk,ckdf->fids", filtered, table, precision=lax.Precision.HIGHEST
    ).astype(jnp.bfloat16)
    turned = lax.all_to_all(spectra, "inp", split_axis=0, concat_axis=1, tiled=True)
    local_channels, all_inputs = (turned.shape[0], turned.shape[1])
    time_shards = lax.axis_size("tm")
    rows_count = all_inputs // time_shards
    total_spectra = local_spectra * time_shards
    first_row = lax.axis_index("tm") * rows_count
    piece = lax.all_gather(turned, "tm", axis=3, tiled=True)
    width = piece.shape[3]
    all_rows = piece.reshape(local_channels, all_inputs, 2 * width)
    my_rows = lax.dynamic_slice_in_dim(piece, first_row, rows_count, 1)
    row_block = my_rows.reshape(local_channels, rows_count, 2 * width)
    swapped = jnp.concatenate([my_rows[:, :, 1, :], -my_rows[:, :, 0, :]], axis=2)
    gram_real = jnp.einsum("fas,fbs->fab", row_block, all_rows, preferred_element_type=jnp.float32)
    gram_imag = jnp.einsum("fas,fbs->fab", swapped, all_rows, preferred_element_type=jnp.float32)
    gram_real, gram_imag = (gram_real, gram_imag)
    result = jnp.concatenate([gram_real, gram_imag], axis=2) * (1.0 / total_spectra)
    return result


def solution(mesh):
    in_specs = (P("inp", None, "tm"), P("inp"), P())
    out_specs = P("inp", "tm", None)
    return jax.shard_map(shards, mesh=mesh, in_specs=in_specs, out_specs=out_specs, check_vma=False)
```

profile of v0, /device:TPU:11, one launch (start us, length us, event | category | flops | bytes accessed | tf_op | source)
XLA Modules:
  0.0 553.4 jit_solution(17232922909311961384)
XLA Ops:
  6.5 3.9 fusion.39
  17.3 18.6 %collective-permute-done = bf16[72,2,3840]{2,1,0:T(2,128)(2,1)} collective-permute-done((bf16[72,2,3840]{2,1,0:T(2,128)(2,1)}, bf16[72,2,3840]{2,1,0:T(2,128)(2,1)}, u32[]{:S(2)}, u32[]{:S(2)}) %collective-permute-start) | collective-permute-done | bytes 1105952 | tf_op jit(solution)/shard_map/ppermute | solution.py:16
  37.4 7.7 %pad_maximum_fusion = bf16[72,2,13824]{2,1,0:T(2,128)(2,1)} fusion(bf16[72,2,3840]{2,1,0:T(2,128)(2,1)} %collective-permute-done.1, bf16[72,2,6144]{2,1,0:T(2,128)(2,1)S(1)} %copy-done, bf16[72,2,3840]{2,1,0:T(2,128)(2,1)} %collective-permute-done), kind=kLoop, calls=%fused_computation.3 | loop fusion | flops 11943936 | bytes 7962624 | tf_op jit(solution)/shard_map/concatenate | solution.py:18
  45.1 235.5 %while.1 = (s32[]{:T(128)}, bf16[72,2,13824]{2,1,0:T(2,128)(2,1)}, s32[72,3]{0,1:T(4,128)S(1)}, bf16[72,2,9984]{2,1,0:T(2,128)(2,1)}, s32[]{:T(128)}) while((s32[]{:T(128)}, bf16[72,2,13824]{2,1,0:T(2,128)(2,1)}, s32[72,3]{0,1:T(4,128)S(1)}, bf16[72,2,9984]{2,1,0:T(2,128)(2,1)}, s32[]{:T(128)}) %tuple.52), condition=%wide.while_cond, body=%wide.while_body.sunk | while | flops 2 | bytes 81513 | solution.py:43
  81.7 2.7 dynamic-slice_dynamic-update-slice_fusion.2
  114.4 2.7 dynamic-slice_dynamic-update-slice_fusion.2
  199.4 2.7 dynamic-slice_dynamic-update-slice_fusion.2
  222.3 2.7 dynamic-slice_dynamic-update-slice_fusion.2
  274.6 2.7 dynamic-slice_dynamic-update-slice_fusion.2
  280.6 7.7 %reshape.60 = f32[72,2,39,256]{3,2,1,0:T(8,128)} reshape(bf16[72,2,9984]{2,1,0:T(2,128)(2,1)} %get-tuple-element.12) | data formatting | bytes 8626176 | tf_op jit(solution)/shard_map/convert_element_type | solution.py:45
  288.3 38.8 %fusion.38 = (f32[72,2,24,256]{3,2,1,0:T(8,128)S(1)}, f32[72,2,24,256]{3,2,1,0:T(8,128)S(1)}, f32[72,2,24,256]{3,2,1,0:T(8,128)S(1)}, f32[72,2,24,256]{3,2,1,0:T...) fusion(f32[72,2,39,256]{3,2,1,0:T(8,128)} %reshape.60), kind=kLoop, calls=%fused_computation.68 | loop fusion | bytes 113246208 | tf_op jit(solution)/shard_map/slice | solution.py:53
  327.1 15.1 %fusion = f32[72,2,24,256]{3,2,0,1:T(8,128)S(1)} fusion(f32[72,2,24,256]{3,2,1,0:T(8,128)} %get-tuple-element.40, f32[72,2,24,256]{3,2,1,0:T(8,128)S(1)} %get-tuple-element.26, f32[72,2,24,256]{3,2,1,0:T(8,128)S(1)} %get-tuple-element.27, f32[72,2,24,256]{3,2,1,0:T(8,128)} %get-tuple-element.28, f32[72,2,24,256]{3,2,1,0:T(8,128)} %get-tuple-element.29, ...), kind=kLoop, calls=%fused_computation.5 | loop fusion | flops 27426816 | bytes 60178432 | tf_op jit(solution)/shard_map/add | solution.py:52
  342.2 7.2 %fusion.22 = bf16[256,72,2,24]{0,1,3,2:T(8,128)(2,1)} fusion(f32[72,2,24,256]{3,2,0,1:T(8,128)S(1)} %fusion, f32[2,256,2,256,1]{3,2,1,0,4:T(2,128)S(1)} %bitcast.55), kind=kOutput, calls=%fused_computation.43 | convolution fusion | flops 5436702720 | bytes 6356992 | tf_op jit(solution)/shard_map/icsk,ckdf->fids/dot_general | solution.py:56
  349.4 3.4 copy.40
  352.8 73.7 %all_to_all.18 = bf16[256,72,2,24]{1,3,2,0:T(8,128)(2,1)S(1)} all-to-all(bf16[256,72,2,24]{1,3,2,0:T(8,128)(2,1)S(1)} %copy.40), channel_id=1, replica_groups=mesh['inp'=8,'tm'=4] {'inp'}, dimensions={0} | all-to-all | bytes 3538944 | tf_op jit(solution)/shard_map/all_to_all | solution.py:59
  428.6 3.3 reshape.61
  431.9 57.4 %all-gather.2.cloned.1.call-done = bf16[32,576,2,96]{1,0,2,3:T(8,128)(2,1)} async-done(((bf16[32,576,2,24]{1,0,2,3:T(8,128)(2,1)}), bf16[32,576,2,96]{1,0,2,3:T(8,128)(2,1)}) %all-gather.2.cloned.1.call-update) | async-done | bytes 7077904 | tf_op jit(solution)/shard_map/all_gather | solution.py:65
  489.3 3.9 constant_dynamic-slice_fusion.2
  493.3 5.5 copy.44
  498.8 5.8 %reshape.31 = bf16[32,144,192]{2,1,0:T(8,128)(2,1)} reshape(bf16[32,144,2,96]{3,2,1,0:T(2,128)(2,1)} %copy.44) | data formatting | bytes 3538944 | tf_op jit(solution)/shard_map/reshape | solution.py:69
  504.6 4.0 constant_dynamic-slice_fusion.1
  515.0 7.8 %copy.45 = bf16[32,576,2,96]{1,3,2,0:T(8,128)(2,1)S(1)} copy(bf16[32,576,2,96]{1,0,2,3:T(8,128)(2,1)} %all-gather.2.cloned.1.call-done) | data formatting | bytes 14155776 | tf_op jit(solution)/shard_map/all_gather | solution.py:65
  522.8 8.1 %fusion.41 = f32[32,144,576]{2,1,0:T(8,128)} fusion(bf16[32,144,192]{2,1,0:T(8,128)(2,1)} %reshape.31, bf16[32,576,192]{1,2,0:T(8,128)(2,1)S(1)} %bitcast.51), kind=kOutput, calls=%fused_computation.71 | convolution fusion | flops 1019215872 | bytes 19464192 | tf_op jit(solution)/shard_map/fas,fbs->fab/dot_general | solution.py:71
  533.1 13.5 %maximum_multiply_fusion = f32[32,144,1152]{2,1,0:T(8,128)} fusion(f32[32,144,576]{2,1,0:T(8,128)S(1)} %fusion.18, f32[32,144,576]{2,1,0:T(8,128)} %fusion.41), kind=kLoop, calls=%fused_computation.2 | loop fusion | flops 10616832 | bytes 42467328 | tf_op jit(solution)/shard_map/mul | solution.py:74
  (239 shorter events, 240.8 us)
Async XLA Ops:
  6.5 30.9 %copy-start = (bf16[72,2,6144]{2,1,0:T(2,128)(2,1)S(1)}, bf16[72,2,6144]{2,1,0:T(2,128)(2,1)}, u32[]{:S(2)}) copy-start(bf16[72,2,6144]{2,1,0:T(2,128)(2,1)} %param.3) | copy-start | bytes 5308420
  6.5 10.7 %copy-start.3 = (s32[72]{0:T(128)S(1)}, s32[72]{0:T(128)}, u32[]{:S(2)}) copy-start(s32[72]{0:T(128)} %param.4) | copy-start | bytes 868
  6.5 10.7 %copy-start.2 = (s32[16,256]{1,0:T(8,128)S(1)}, s32[16,256]{1,0:T(8,128)}, u32[]{:S(2)}) copy-start(s32[16,256]{1,0:T(8,128)} %param.5) | copy-start | bytes 49156
  6.5 482.8 %all-gather.2.cloned.1.call-start = ((), (), s32[]{:S(2)}) async-start(), calls=%async_computation.1 | async-start | bytes 9830400 | tf_op jit(solution)/shard_map/all_gather | solution.py:65
  10.4 25.5 %collective-permute-start = (bf16[72,2,3840]{2,1,0:T(2,128)(2,1)}, bf16[72,2,3840]{2,1,0:T(2,128)(2,1)}, u32[]{:S(2)}, u32[]{:S(2)}) collective-permute-start(bf16[72,2,3840]{2,1,0:T(2,128)(2,1)} %get-tuple-element.41), channel_id=1, source_target_pairs={{0,1},{1,2},{2,3},{3,0},{4,5},{5,6},{6,7},{7,4},{8,9},{9,10},{10,1... | collective-permute-start | bytes 3317768 | tf_op jit(solution)/shard_map/ppermute | solution.py:16
  12.2 25.2 %collective-permute-start.1 = (bf16[72,2,3840]{2,1,0:T(2,128)(2,1)}, bf16[72,2,3840]{2,1,0:T(2,128)(2,1)}, u32[]{:S(2)}, u32[]{:S(2)}) collective-permute-start(bf16[72,2,3840]{2,1,0:T(2,128)(2,1)} %get-tuple-element.42), channel_id=1, source_target_pairs={{1,0},{2,1},{3,2},{0,3},{5,4},{6,5},{7,6},{4,7},{9,8},{10,9},{11,1... | collective-permute-start | bytes 3317768 | tf_op jit(solution)/shard_map/ppermute | solution.py:17
  522.8 8.2 %copy-start.1 = (bf16[32,144,1,96]{3,1,0,2:T(8,128)(2,1)S(1)}, bf16[32,144,1,96]{3,1,0,2:T(8,128)(2,1)}, u32[]{:S(2)}) copy-start(bf16[32,144,1,96]{3,1,0,2:T(8,128)(2,1)} %copy.71) | copy-start | bytes 2654212
Sparse Core Ops, SparseCore 0:
  432.0 57.2 all-gather.1
where the time goes:
time: 561 us; the launch traced here: 553 us
  local copies, waits for them, and re-layouts  328 us (58%)
  waiting for transfers between devices  77.5 us (14%)
  blocking collectives  73.7 us (13%)
  other arithmetic  40.9 us (7%)
  matrix products  17.5 us (3%)
  between operations  13.5 us (2%)
    gather x216, local copies, waits for them, and re-layouts  235 us
    all_to_all x1, blocking collectives, shards(): lax.all_to_all(spectra, 'inp', split_axis=0, concat_axis=1, tiled=True)  73.7 us
    all_gather x1, waiting for transfers between devices, shards(): piece = lax.all_gather(turned, 'tm', axis=3, tiled=True)  57.4 us
    slice x1, local copies, waits for them, and re-layouts, shards(): frames[:, :, begin:begin + local_spectra, :]  38.8 us
    ppermute x1, waiting for transfers between devices, with_halo(): before = lax.ppermute(last, axis, up)  18.6 us
    add x1, other arithmetic, shards(): filtered + coefficient[tap][None, None, None, :] * frames[:, :, begin:beg...  15.1 us
    mul x1, other arithmetic, shards(): jnp.concatenate([gram_real, gram_imag], axis=2) * (1.0 / total_spectra)  13.5 us
  transfers between devices with their start and end apart: 3, of which 3 were waited for; matrix products, arithmetic and copies ran while one was open for 1% of the time, Pallas kernels for 0%

commit v1 on v0

v1 whole, which is shorter than its diff:
```python
import functools
import math

import jax
import jax.numpy as jnp
import numpy as np
from jax import lax
from jax.experimental import pallas as pl
from jax.experimental.pallas import tpu as pltpu
from jax.sharding import PartitionSpec as P

LANES = 128
GROUP = 8


def dft_tables(length, groups):
    index = np.arange(length)
    phase = (np.outer(index, index) % length) * (2.0 * math.pi / length)
    cosine, sine = np.cos(phase), np.sin(phase)
    table = np.stack([np.stack([cosine, -sine]), np.stack([sine, cosine])])
    table = table.transpose(0, 2, 1, 3).reshape(2 * length, 2, groups, length // groups)
    table = table.transpose(0, 2, 1, 3).reshape(2 * length, 2 * length) / math.sqrt(length)
    high = table.astype(jnp.bfloat16)
    low = (table - high.astype(np.float64)).astype(jnp.bfloat16)
    return high, low


def spectra_kernel(dims, delays_ref, before_ref, own_ref, after_ref, coef_ref, high_ref, low_ref, out_ref, flat, slab, filt):
    tap_count, parts, spectra, hist, skip = dims
    own = own_ref.shape[2]
    groups = out_ref.shape[0]
    frames = spectra + tap_count - 1
    need = -(-frames * parts // GROUP) * GROUP
    step = pl.program_id(0)
    lane = lax.broadcasted_iota(jnp.int32, (need, LANES), 1)
    for c in range(2):
        for j in range(GROUP):
            delay = delays_ref[step * GROUP + j]
            rows, shift = delay // LANES, delay % LANES
            turn = lax.rem(LANES - shift, LANES)
            buf = flat.at[(c * GROUP + j) % flat.shape[0]]
            buf[0:hist, :] = pltpu.roll(before_ref[j, c].astype(jnp.float32), turn, 1)
            buf[hist : hist + own, :] = pltpu.roll(own_ref[j, c].astype(jnp.float32), turn, 1)
            buf[hist + own : hist + own + hist, :] = pltpu.roll(after_ref[j, c].astype(jnp.float32), turn, 1)
            low = buf[pl.ds(rows + skip, need), :]
            high = buf[pl.ds(rows + skip + 1, need), :]
            slab[c, pl.ds(j, need, stride=GROUP), :] = jnp.where(lane < LANES - shift, low, high)
    block = 8
    for c in range(2):
        for h in range(parts):
            for s0 in range(0, spectra, block):
                taps = [coef_ref[m, h] for m in range(tap_count)]
                held = {}
                for s in range(s0, min(s0 + block, spectra)):
                    total = None
                    for m in range(tap_count):
                        row = parts * (s + tap_count - 1 - m) + h
                        if row not in held:
                            held[row] = slab[c, row * GROUP : (row + 1) * GROUP, :]
                        term = taps[m] * held[row]
                        total = term if total is None else total + term
                    filt[s * GROUP : (s + 1) * GROUP, (c * parts + h) * LANES : (c * parts + h + 1) * LANES] = total
    value = filt[...]
    high = value.astype(jnp.bfloat16)
    low = (value - high.astype(jnp.float32)).astype(jnp.bfloat16)
    result = (
        jnp.dot(high, high_ref[...], preferred_element_type=jnp.float32)
        + jnp.dot(low, high_ref[...], preferred_element_type=jnp.float32)
        + jnp.dot(high, low_ref[...], preferred_element_type=jnp.float32)
    )
    width = result.shape[1] // groups
    packs = LANES // width
    rows = spectra * GROUP // packs
    place = lax.broadcasted_iota(jnp.int32, (rows, LANES), 1) // width
    for p in range(groups // packs):
        pieces = [result[j * rows : (j + 1) * rows, p * LANES : (p + 1) * LANES] for j in range(packs)]
        for q in range(packs):
            total = pieces[q]
            for j in range(packs):
                if j != q:
                    moved = pltpu.roll(pieces[j], ((j - q) * width) % LANES, 1)
                    total = jnp.where(place == j, moved, total)
            out_ref[p * packs + q, 0] = total.astype(jnp.bfloat16)


def gram_kernel(scale, which_ref, x_ref, out_ref, mine):
    shards, _, depth, inputs = x_ref.shape
    rows = out_ref.shape[1]
    half = depth // 2
    x = x_ref[...].reshape(shards * depth, inputs)
    for t in range(inputs // rows):

        @pl.when(which_ref[0] == t)
        def _():
            mine[...] = x[:, t * rows : (t + 1) * rows].astype(jnp.float32)

    left = mine[...]
    turned = []
    for t in range(shards):
        turned.append(left[t * depth + half : (t + 1) * depth])
        turned.append(-left[t * depth : t * depth + half])
    turned = jnp.concatenate(turned, axis=0).astype(jnp.bfloat16)
    dims = (((0,), (0,)), ((), ()))
    real = lax.dot_general(left.astype(jnp.bfloat16), x, dims, preferred_element_type=jnp.float32)
    imag = lax.dot_general(turned, x, dims, preferred_element_type=jnp.float32)
    out_ref[0, :, 0:inputs] = real * scale
    out_ref[0, :, inputs : 2 * inputs] = imag * scale


def front(samples, delays, taps):
    tap_count, channels = taps.shape
    local_inputs, _, shard_len = samples.shape
    peers = lax.axis_size("tm")
    groups = lax.axis_size("inp")
    parts = channels // LANES
    spectra = shard_len // channels
    margin_rows = (tap_count - 1) * parts
    hist = -(-margin_rows // 16) * 16
    own = shard_len // LANES
    lined = samples.reshape(local_inputs, 2, own, LANES)
    up = [(i, (i + 1) % peers) for i in range(peers)]
    down = [(j, i) for i, j in up]
    before = lax.ppermute(lined[:, :, own - hist :], "tm", up)
    after = lax.ppermute(lined[:, :, :hist], "tm", down)
    steps = -(-local_inputs // GROUP)
    offsets = jnp.pad(delays, (0, steps * GROUP - local_inputs))
    coef = (taps.astype(jnp.float32) * (1.0 / 4096.0)).reshape(tap_count, parts, 1, LANES)
    coef = jnp.broadcast_to(coef, (tap_count, parts, GROUP, LANES))
    high, low = dft_tables(channels, groups)
    width = 2 * channels // groups
    packs = LANES // width
    rows = spectra * GROUP // packs
    need = -(-(spectra + tap_count - 1) * parts // GROUP) * GROUP
    total = -(-max(2 * hist + own, need + hist + 1) // GROUP) * GROUP
    fixed = lambda shape: pl.BlockSpec(shape, lambda i, d: (0,) * len(shape))
    return pl.pallas_call(
        functools.partial(spectra_kernel, (tap_count, parts, spectra, hist, hist - margin_rows)),
        out_shape=jax.ShapeDtypeStruct((groups, steps, rows, LANES), jnp.bfloat16),
        grid_spec=pltpu.PrefetchScalarGridSpec(
            num_scalar_prefetch=1,
            grid=(steps,),
            in_specs=[
                pl.BlockSpec((GROUP, 2, hist, LANES), lambda i, d: (i, 0, 0, 0)),
                pl.BlockSpec((GROUP, 2, own, LANES), lambda i, d: (i, 0, 0, 0)),
                pl.BlockSpec((GROUP, 2, hist, LANES), lambda i, d: (i, 0, 0, 0)),
                fixed(coef.shape),
                fixed(high.shape),
                fixed(low.shape),
            ],
            out_specs=pl.BlockSpec((groups, 1, rows, LANES), lambda i, d: (0, i, 0, 0)),
            scratch_shapes=[
                pltpu.VMEM((4, total, LANES), jnp.float32),
                pltpu.VMEM((2, need * GROUP, LANES), jnp.float32),
                pltpu.VMEM((spectra * GROUP, 2 * channels), jnp.float32),
            ],
        ),
        name="spectra",
    )(offsets, before, lined, after, coef, jnp.asarray(high), jnp.asarray(low))


def gram(gathered, rows, scale):
    shards, channels, depth, inputs = gathered.shape
    which = lax.axis_index("tm").astype(jnp.int32).reshape(1)
    return pl.pallas_call(
        functools.partial(gram_kernel, scale),
        out_shape=jax.ShapeDtypeStruct((channels, rows, 2 * inputs), jnp.float32),
        grid_spec=pltpu.PrefetchScalarGridSpec(
            num_scalar_prefetch=1,
            grid=(channels,),
            in_specs=[pl.BlockSpec((shards, 1, depth, inputs), lambda f, w: (0, f, 0, 0))],
            out_specs=pl.BlockSpec((1, rows, 2 * inputs), lambda f, w: (f, 0, 0)),
            scratch_shapes=[pltpu.VMEM((shards * depth, rows), jnp.float32)],
        ),
        name="gram",
    )(which, gathered)


def shards(samples, delays, taps):
    channels = taps.shape[1]
    local_inputs, _, shard_len = samples.shape
    groups, peers = lax.axis_size("inp"), lax.axis_size("tm")
    inputs = local_inputs * groups
    spectra = shard_len // channels
    mine = channels // groups
    packs = LANES // (2 * mine)
    sent = front(samples, delays, taps)
    turned = lax.all_to_all(sent, "inp", split_axis=0, concat_axis=0, tiled=True)
    steps = turned.shape[1]
    turned = turned.reshape(groups, steps, spectra // packs, GROUP, packs, 2, mine)
    turned = turned.transpose(6, 5, 4, 2, 0, 1, 3).reshape(mine, 2 * spectra, groups, steps * GROUP)
    turned = turned[..., :local_inputs].reshape(mine, 2 * spectra, inputs)
    gathered = lax.all_gather(turned, "tm", axis=0, tiled=False)
    return gram(gathered, inputs // peers, 1.0 / (spectra * peers))


def solution(mesh):
    in_specs = (P("inp", None, "tm"), P("inp"), P())
    out_specs = P("inp", "tm", None)
    return jax.shard_map(shards, mesh=mesh, in_specs=in_specs, out_specs=out_specs, check_vma=False)
```

time: 561 us -> 217 us (0.39)
  local copies, waits for them, and re-layouts: 328 us -> 28.2 us
  Pallas kernels: 0 us -> 44 us
  other arithmetic: 40.9 us -> 0.6 us
  blocking collectives: 73.7 us -> 43.9 us
  matrix products: 17.5 us -> 0 us
    gather x216 -> x0, local copies, waits for them, and re-layouts: 235 us -> none
    slice x4 -> x1, local copies, waits for them, and re-layouts: 46.7 us -> 1.74 us  [front(): after = lax.ppermute(lined[:, :, :hist], 'tm', down)]
    pallas_call x0 -> x2, Pallas kernels: none -> 44 us  [the longest x1 29.3 us: gram(): pl.pallas_call(functools.partial(gram_kernel, scale), out_shape=jax.Shape...]
    all_to_all x1, blocking collectives: 73.7 us -> 43.9 us  [shards(): lax.all_to_all(sent, 'inp', split_axis=0, concat_axis=0, tiled=True)]
    dot_general x3 -> x0, matrix products: 17.5 us -> none  [the longest x1 8.15 us: shards(): jnp.einsum('fas,fbs->fab', row_block, all_rows, preferred_element_type=jn...]
    add x1 -> x0, other arithmetic: 15.1 us -> none  [shards(): filtered + coefficient[tap][None, None, None, :] * frames[:, :, begin:beg...]
    mul x2 -> x1, other arithmetic: 13.5 us -> 0.6 us  [front(): taps.astype(jnp.float32) * (1.0 / 4096.0)]
    reshape x1 -> x3, local copies, waits for them, and re-layouts: 5.85 us -> 17.4 us  [the longest x2 13.1 us: shards(): turned.reshape(groups, steps, spectra // packs, GROUP, packs, 2, mine)]
  transfers between devices with their start and end apart: 3 -> 3, of which waited for: 3 -> 2; matrix products, arithmetic and copies ran while one was open for 1% -> 1% of each run, Pallas kernels for 0% -> 0%
where the time goes in v1:
time: 217 us; the launch traced here: 215 us
  waiting for transfers between devices  83.1 us (38%)
  Pallas kernels  44 us (20%)
  blocking collectives  43.9 us (20%)
  local copies, waits for them, and re-layouts  28.2 us (13%)
  between operations  13.4 us (6%)
    all_gather x1, waiting for transfers between devices, shards(): gathered = lax.all_gather(turned, 'tm', axis=0, tiled=False)  58.1 us
    all_to_all x1, blocking collectives, shards(): lax.all_to_all(sent, 'inp', split_axis=0, concat_axis=0, tiled=True)  43.9 us
    pallas_call x1, Pallas kernels, gram(): pl.pallas_call(functools.partial(gram_kernel, scale), out_shape=jax.Shape...  29.3 us
    ppermute x1, waiting for transfers between devices, front(): after = lax.ppermute(lined[:, :, :hist], 'tm', down)  25 us
    pallas_call x1, Pallas kernels, front(): pl.pallas_call(functools.partial(spectra_kernel, (tap_count, parts, spect...  14.8 us
    reshape x2, local copies, waits for them, and re-layouts, shards(): turned.reshape(groups, steps, spectra // packs, GROUP, packs, 2, mine)  13.1 us
    another operation x1, local copies, waits for them, and re-layouts, shards(): gathered = lax.all_gather(turned, 'tm', axis=0, tiled=False)  6.88 us
  transfers between devices with their start and end apart: 3, of which 2 were waited for; matrix products, arithmetic and copies ran while one was open for 1% of the time, Pallas kernels for 0%

profile of v1, /device:TPU:11, one launch (start us, length us, event | category | flops | bytes accessed | tf_op | source)
XLA Modules:
  0.0 215.0 jit_solution(204058741169713660)
XLA Ops:
  6.5 0.0 all-gather.2.cloned.1.call-start
  6.5 4.3 %reshape.12.own_ref = bf16[72,2,48,128]{3,2,1,0:T(8,128)(2,1)S(1)} reshape(bf16[72,2,6144]{2,1,0:T(2,128)(2,1)} %param.5) | data formatting | bytes 3538944 | tf_op jit(solution)/shard_map/reshape | solution.py:120
  10.8 0.0 copy-start
  10.8 0.0 copy-start.3
  10.9 1.7 fusion
  12.6 0.0 copy-done
  12.6 0.7 collective-permute-start.1
  13.3 1.1 collective-permute-start
  14.4 0.0 copy-done.3
  14.4 0.6 convert_multiply_fusion
  15.0 0.7 broadcast_in_dim.7
  15.7 25.0 %collective-permute-done.1.after_ref = bf16[72,2,32,128]{3,2,1,0:T(8,128)(2,1)S(1)} collective-permute-done((bf16[72,2,32,128]{3,2,1,0:T(8,128)(2,1)}, bf16[72,2,32,128]{3,2,1,0:T(8,128)(2,1)S(1)}, u32[]{:S(2)}, u32[]{:S(2)}) %collective-permute-start.1) | collective-permute-done | bytes 1179680 | tf_op jit(solution)/shard_map/ppermute | solution.py:124
  40.8 0.0 collective-permute-done.before_ref
  40.8 0.7 broadcast_in_dim.8.coef_ref
  41.5 0.3 copy-done.1
  41.8 0.4 copy-done.2
  42.2 14.8 %spectra.1 = bf16[8,9,96,128]{3,2,1,0:T(8,128)(2,1)} custom-call(s32[72]{0:T(128)} %delays_ref.1, bf16[72,2,32,128]{3,2,1,0:T(8,128)(2,1)} %copy-done.2, bf16[72,2,48,128]{3,2,1,0:T(8,128)(2,1)} %copy-done, bf16[72,2,32,128]{3,2,1,0:T(8,128)(2,1)} %copy-done.1, f32[16,2,8,128]{3,2,1,0:T(8,128)} %broadcast_in_dim.8.coef_ref, ...), custom_call_target="tpu_custom_call" | custom-call | tf_op jit(solution)/shard_map/spectra/pallas_call | solution.py:136
  56.9 43.9 %all_to_all.5 = bf16[8,9,96,128]{3,2,1,0:T(8,128)(2,1)S(1)} all-to-all(bf16[8,9,96,128]{3,2,1,0:T(8,128)(2,1)} %spectra.1), channel_id=1, replica_groups=mesh['inp'=8,'tm'=4] {'inp'}, dimensions={0} | all-to-all | bytes 3538944 | tf_op jit(solution)/shard_map/all_to_all | solution.py:187
  100.8 5.4 %reshape.13 = bf16[8,9,12,8,2,2,32]{6,5,4,3,2,1,0:T(2,128)(2,1)} reshape(bf16[8,9,96,128]{3,2,1,0:T(8,128)(2,1)S(1)} %all_to_all.5) | data formatting | bytes 3538944 | tf_op jit(solution)/shard_map/reshape | solution.py:189
  106.2 7.7 %copy.9 = bf16[8,9,12,8,2,2,32]{6,3,1,0,2,4,5:T(8,128)(2,1)} copy(bf16[8,9,12,8,2,2,32]{6,5,4,3,2,1,0:T(2,128)(2,1)} %reshape.13) | data formatting | bytes 3538944 | tf_op jit(solution)/shard_map/reshape | solution.py:189
  113.9 6.9 %copy.10 = bf16[1,32,48,576]{3,2,1,0:T(8,128)(2,1)} copy(bf16[1,32,48,576]{1,3,2,0:T(8,128)(2,1)} %bitcast.6) | data formatting | bytes 3538944 | tf_op jit(solution)/shard_map/all_gather;reshape;reshape | solution.py:192
  120.8 0.0 all-gather.2.cloned.1.call-update
  120.8 58.1 %all-gather.2.cloned.1.call-done.x_ref = bf16[4,32,48,576]{3,2,1,0:T(8,128)(2,1)} async-done(((bf16[1,32,48,576]{3,2,1,0:T(8,128)(2,1)}), bf16[4,32,48,576]{3,2,1,0:T(8,128)(2,1)}) %all-gather.2.cloned.1.call-update) | async-done | bytes 7077904 | tf_op jit(solution)/shard_map/all_gather | solution.py:192
  178.9 29.3 %gram.1 = f32[32,144,1152]{2,1,0:T(8,128)} custom-call(s32[1]{0:T(128)} %bitcast.which_ref, bf16[4,32,48,576]{3,2,1,0:T(8,128)(2,1)} %all-gather.2.cloned.1.call-done.x_ref), custom_call_target="tpu_custom_call" | custom-call | tf_op jit(solution)/shard_map/gram/pallas_call | solution.py:164
  (2 shorter events, 0.0 us)
Async XLA Ops:
  6.5 172.4 %all-gather.2.cloned.1.call-start = ((), (), s32[]{:S(2)}) async-start(), calls=%async_computation.1 | async-start | bytes 9830400 | tf_op jit(solution)/shard_map/all_gather | solution.py:192
  10.8 1.8 copy-start
  10.8 3.6 %copy-start.3 = (s32[16,256]{1,0:T(8,128)S(1)}, s32[16,256]{1,0:T(8,128)}, u32[]{:S(2)}) copy-start(s32[16,256]{1,0:T(8,128)} %param.7) | copy-start | bytes 49156
  12.6 28.2 %collective-permute-start.1 = (bf16[72,2,32,128]{3,2,1,0:T(8,128)(2,1)}, bf16[72,2,32,128]{3,2,1,0:T(8,128)(2,1)S(1)}, u32[]{:S(2)}, u32[]{:S(2)}) collective-permute-start(bf16[72,2,32,128]{3,2,1,0:T(8,128)(2,1)} %get-tuple-element.5), channel_id=1, source_target_pairs={{1,0},{2,1},{3,2},{0,3},{5,4},{6,5},{7,6},{4,7},{9,8},{10,9},{11,1... | collective-permute-start | bytes 3538952 | tf_op jit(solution)/shard_map/ppermute | solution.py:124
  13.3 27.5 %collective-permute-start = (bf16[72,2,32,128]{3,2,1,0:T(8,128)(2,1)S(1)}, bf16[72,2,32,128]{3,2,1,0:T(8,128)(2,1)S(1)}, u32[]{:S(2)}, u32[]{:S(2)}) collective-permute-start(bf16[72,2,32,128]{3,2,1,0:T(8,128)(2,1)S(1)} %get-tuple-element.6), channel_id=1, source_target_pairs={{0,1},{1,2},{2,3},{3,0},{4,5},{5,6},{6,7},{7,4},{8,9},{9,10},{10,1... | collective-permute-start | bytes 3538952 | tf_op jit(solution)/shard_map/ppermute | solution.py:123
  40.8 1.1 copy-start.1
  40.8 1.4 copy-start.2
Sparse Core Ops, SparseCore 0:
  120.9 57.9 all-gather.1

commit v2 on v1

--- a/solution.py
+++ b/solution.py
@@ -11,6 +11,7 @@
 
 LANES = 128
 GROUP = 8
+CORES = 2
 
 
 def dft_tables(length, groups):
@@ -175,6 +176,181 @@
     )(which, gathered)
 
 
+def exchange_kernel(sent_ref, out_ref, own_sem, turn_send, turn_recv, far_send, far_recv, near_send, near_recv, pass_send, pass_recv):
+    groups, peers = lax.axis_size("inp"), lax.axis_size("tm")
+    chips = peers // CORES
+    g, t = lax.axis_index("inp"), lax.axis_index("tm")
+    y, core = t // CORES, t % CORES
+    partner = y * CORES + (CORES - 1 - core)
+
+    def far(step):
+        return ((y + step) % chips) * CORES + core
+
+    def back(step):
+        return ((y + chips - step) % chips) * CORES + core
+
+    def remote(src, dst, send, recv, to_g, to_t):
+        return pltpu.make_async_remote_copy(
+            src_ref=src, dst_ref=dst, send_sem=send, recv_sem=recv,
+            device_id={"inp": to_g, "tm": to_t}, device_id_type=pl.DeviceIdType.MESH,
+        )
+
+    barrier = pltpu.get_barrier_semaphore()
+    for o in range(1, groups):
+        pl.semaphore_signal(barrier, inc=1, device_id={"inp": (g + o) % groups, "tm": t}, device_id_type=pl.DeviceIdType.MESH)
+    for step in range(1, chips):
+        pl.semaphore_signal(barrier, inc=1, device_id={"inp": g, "tm": far(step)}, device_id_type=pl.DeviceIdType.MESH)
+    pl.semaphore_signal(barrier, inc=1, device_id={"inp": g, "tm": partner}, device_id_type=pl.DeviceIdType.MESH)
+    pl.semaphore_wait(barrier, groups - 1 + chips - 1 + 1)
+
+    def turn(o):
+        to = (g + o) % groups
+        return remote(sent_ref.at[to], out_ref.at[t, g], turn_send.at[o], turn_recv.at[o], to, t)
+
+    def slot(o):
+        return out_ref.at[t, (g + groups - o) % groups]
+
+    def spread(o, src):
+        dst = slot(o)
+        copies = [remote(src, dst, far_send.at[step, o], far_recv.at[step, o], g, far(step)) for step in range(1, chips)]
+        return copies + [remote(src, dst, near_send.at[o], near_recv.at[o], g, partner)]
+
+    def relay(step, o):
+        piece = out_ref.at[back(step), (g + groups - o) % groups]
+        return remote(piece, piece, pass_send.at[step, o], pass_recv.at[step, o], g, partner)
+
+    order = list(range(1, groups))
+    for o in order:
+        turn(o).start()
+    own = pltpu.make_async_copy(sent_ref.at[g], out_ref.at[t, g], own_sem)
+    own.start()
+    for copy in spread(0, sent_ref.at[g]):
+        copy.start()
+
+    def land(o):
+        for step in range(1, chips):
+            piece = out_ref.at[back(step), (g + groups - o) % groups]
+            remote(piece, piece, far_send.at[step, o], far_recv.at[step, o], g, far(step)).wait_recv()
+            relay(step, o).start()
+
+    previous = 0
+    for o in order:
+        turn(o).wait_recv()
+        for copy in spread(o, slot(o)):
+            copy.start()
+        land(previous)
+        previous = o
+    land(previous)
+    own.wait()
+    for o in range(groups):
+        if o:
+            turn(o).wait_send()
+        src = slot(o) if o else sent_ref.at[g]
+        for copy in spread(o, src):
+            copy.wait_send()
+        piece = out_ref.at[partner, (g + groups - o) % groups]
+        remote(piece, piece, near_send.at[o], near_recv.at[o], g, partner).wait_recv()
+        for step in range(1, chips):
+            relay(step, o).wait_send()
+            other = ((y + chips - step) % chips) * CORES + (CORES - 1 - core)
+            piece = out_ref.at[other, (g + groups - o) % groups]
+            remote(piece, piece, pass_send.at[step, o], pass_recv.at[step, o], g, partner).wait_recv()
+
+
+def exchange(sent):
+    groups, peers = lax.axis_size("inp"), lax.axis_size("tm")
+    chips = peers // CORES
+    dma = pltpu.SemaphoreType.DMA
+    return pl.pallas_call(
+        exchange_kernel,
+        out_shape=jax.ShapeDtypeStruct((peers,) + sent.shape, sent.dtype),
+        in_specs=[pl.BlockSpec(memory_space=pl.ANY)],
+        out_specs=pl.BlockSpec(memory_space=pl.ANY),
+        scratch_shapes=[
+            dma, dma((groups,)), dma((groups,)), dma((chips, groups)), dma((chips, groups)),
+            dma((groups,)), dma((groups,)), dma((chips, groups)), dma((chips, groups)),
+        ],
+        compiler_params=pltpu.CompilerParams(collective_id=0, has_side_effects=True),
+        name="exchange",
+    )(sent)
+
+
+def turned_gram_kernel(scale, channels, which_ref, buf_ref, out_ref, lined, mine):
+    peers, groups, steps, rows, _ = buf_ref.shape
+    inputs = groups * steps * GROUP
+    width = 2 * channels
+    packs = LANES // width
+    depth = lined.shape[1] // channels
+    half = depth // 2
+    spectra = half // peers
+    per_pack = spectra // packs
+    tiles = lined.shape[0]
+    height = out_ref.shape[1]
+    f = pl.program_id(0)
+
+    @pl.when(f == 0)
+    def _():
+        @pl.loop(0, peers * (rows // 16))
+        def _(index):
+            t, pair = index // (rows // 16), index % (rows // 16)
+            block = buf_ref[t, :, :, pl.ds(pl.multiple_of(pair * 16, 16), 16), :].astype(jnp.float32)
+            block = block.reshape(groups * steps, 2, GROUP, LANES)
+            for u in range(2):
+                value = block[:, u].reshape(inputs, LANES)
+                for a in range(tiles):
+                    count = min(LANES, inputs - a * LANES)
+                    moved = value[a * LANES : a * LANES + count].T
+                    for j in range(packs):
+                        for d in range(2):
+                            line = d * half + t * spectra + j * per_pack + pair * 2 + u
+                            first = j * width + d * channels
+                            piece = moved[first : first + channels]
+                            if count == LANES:
+                                lined[a, pl.ds(line, channels, stride=depth), :] = piece
+                            else:
+                                lined[a, pl.ds(line, channels, stride=depth), :] = jnp.concatenate(
+                                    [piece, jnp.zeros((channels, LANES - count), jnp.float32)], axis=1
+                                )
+
+    start = pl.multiple_of(f * depth, 8)
+    x = jnp.concatenate([lined[a, pl.ds(start, depth), :] for a in range(tiles)], axis=1)
+    for t in range(inputs // height):
+
+        @pl.when(which_ref[0] == t)
+        def _():
+            mine[...] = x[:, t * height : (t + 1) * height]
+
+    left = mine[...]
+    other = jnp.concatenate([left[half:], -left[:half]], axis=0)
+    both = jnp.concatenate([left.T, other.T], axis=0).astype(jnp.bfloat16)
+    result = jnp.dot(both, x.astype(jnp.bfloat16), preferred_element_type=jnp.float32) * scale
+    out_ref[0, :, 0:inputs] = result[:height, :inputs]
+    out_ref[0, :, inputs : 2 * inputs] = result[height:, :inputs]
+
+
+def turned_gram(buf, channels, height, scale):
+    peers, groups, steps, rows, _ = buf.shape
+    inputs = groups * steps * GROUP
+    packs = LANES // (2 * channels)
+    depth = 2 * peers * packs * rows // GROUP
+    which = lax.axis_index("tm").astype(jnp.int32).reshape(1)
+    return pl.pallas_call(
+        functools.partial(turned_gram_kernel, scale, channels),
+        out_shape=jax.ShapeDtypeStruct((channels, height, 2 * inputs), jnp.float32),
+        grid_spec=pltpu.PrefetchScalarGridSpec(
+            num_scalar_prefetch=1,
+            grid=(channels,),
+            in_specs=[pl.BlockSpec(buf.shape, lambda f, w: (0, 0, 0, 0, 0), pipeline_mode=pl.Buffered(1))],
+            out_specs=pl.BlockSpec((1, height, 2 * inputs), lambda f, w: (f, 0, 0)),
+            scratch_shapes=[
+                pltpu.VMEM((-(-inputs // LANES), channels * depth, LANES), jnp.float32),
+                pltpu.VMEM((depth, height), jnp.float32),
+            ],
+        ),
+        name="turned_gram",
+    )(which, buf)
+
+
 def shards(samples, delays, taps):
     channels = taps.shape[1]
     local_inputs, _, shard_len = samples.shape
@@ -184,6 +360,8 @@
     mine = channels // groups
     packs = LANES // (2 * mine)
     sent = front(samples, delays, taps)
+    if local_inputs % GROUP == 0 and sent.shape[2] % 16 == 0:
+        return turned_gram(exchange(sent), mine, inputs // peers, 1.0 / (spectra * peers))
     turned = lax.all_to_all(sent, "inp", split_axis=0, concat_axis=0, tiled=True)
     steps = turned.shape[1]
     turned = turned.reshape(groups, steps, spectra // packs, GROUP, packs, 2, mine)

time: 217 us -> 159 us (0.73)
  the two profiles are of different devices: /device:TPU:11 before, /device:TPU:25 now
where the time goes in v2:
time: 159 us
  Pallas kernels  123 us (77%)
  waiting for transfers between devices  25 us (16%)
  local copies, waits for them, and re-layouts  8.25 us (5%)
  starting transfers between devices  1.8 us (1%)
    pallas_call x1, Pallas kernels, exchange(): pl.pallas_call(exchange_kernel, out_shape=jax.ShapeDtypeStruct((peers,) +...  66.9 us
    pallas_call x1, Pallas kernels, turned_gram(): pl.pallas_call(functools.partial(turned_gram_kernel, scale, channels), ou...  41.3 us
    ppermute x1, waiting for transfers between devices, front(): after = lax.ppermute(lined[:, :, :hist], 'tm', down)  25 us
    pallas_call x1, Pallas kernels, front(): pl.pallas_call(functools.partial(spectra_kernel, (tap_count, parts, spect...  14.7 us
    reshape x1, local copies, waits for them, and re-layouts, front(): lined = samples.reshape(local_inputs, 2, own, LANES)  4.29 us
  transfers between devices with their start and end apart: 2, of which 1 were waited for; matrix products, arithmetic and copies ran while one was open for 1% of the time, Pallas kernels for 0%

profile of v2, /device:TPU:25, one launch (start us, length us, event | category | flops | bytes accessed | tf_op | source)
XLA Modules:
  0.0 158.7 jit_solution(15924955933480960974)
XLA Ops:
  0.0 4.3 %reshape.9.own_ref = bf16[72,2,48,128]{3,2,1,0:T(8,128)(2,1)S(1)} reshape(bf16[72,2,6144]{2,1,0:T(2,128)(2,1)} %param.5) | data formatting | bytes 3538944 | tf_op jit(solution)/shard_map/reshape | solution.py:121
  4.3 0.0 copy-start
  4.3 0.0 copy-start.3
  4.3 1.7 %fusion = (bf16[72,2,32,128]{3,2,1,0:T(8,128)(2,1)}, bf16[72,2,32,128]{3,2,1,0:T(8,128)(2,1)S(1)}) fusion(bf16[72,2,48,128]{3,2,1,0:T(8,128)(2,1)S(1)} %reshape.9.own_ref), kind=kLoop, calls=%fused_computation.1 | loop fusion | bytes 4718592 | tf_op jit(solution)/shard_map/slice | solution.py:125
  6.1 0.0 copy-done
  6.1 0.7 collective-permute-start.1
  6.7 1.1 collective-permute-start
  7.9 0.0 copy-done.3
  7.9 0.6 convert_multiply_fusion
  8.5 0.7 broadcast_in_dim.7
  9.2 25.0 %collective-permute-done.1.after_ref = bf16[72,2,32,128]{3,2,1,0:T(8,128)(2,1)S(1)} collective-permute-done((bf16[72,2,32,128]{3,2,1,0:T(8,128)(2,1)}, bf16[72,2,32,128]{3,2,1,0:T(8,128)(2,1)S(1)}, u32[]{:S(2)}, u32[]{:S(2)}) %collective-permute-start.1) | collective-permute-done | bytes 1179680 | tf_op jit(solution)/shard_map/ppermute | solution.py:125
  34.2 0.0 copy-start.1
  34.2 0.0 collective-permute-done.before_ref
  34.2 0.0 copy-start.2
  34.2 0.7 broadcast_in_dim.8.coef_ref
  35.0 0.3 copy-done.1
  35.3 0.4 copy-done.2
  35.7 14.7 %spectra.1.sent_ref = bf16[8,9,96,128]{3,2,1,0:T(8,128)(2,1)} custom-call(s32[72]{0:T(128)} %delays_ref.1, bf16[72,2,32,128]{3,2,1,0:T(8,128)(2,1)} %copy-done.2, bf16[72,2,48,128]{3,2,1,0:T(8,128)(2,1)} %copy-done, bf16[72,2,32,128]{3,2,1,0:T(8,128)(2,1)} %copy-done.1, f32[16,2,8,128]{3,2,1,0:T(8,128)} %broadcast_in_dim.8.coef_ref, ...), custom_call_target="tpu_custom_call" | custom-call | tf_op jit(solution)/shard_map/spectra/pallas_call | solution.py:137
  50.4 66.9 %exchange.1.buf_ref = bf16[4,8,9,96,128]{4,3,2,1,0:T(8,128)(2,1)} custom-call(bf16[8,9,96,128]{3,2,1,0:T(8,128)(2,1)} %spectra.1.sent_ref), custom_call_target="tpu_custom_call" | custom-call | tf_op jit(solution)/shard_map/exchange/pallas_call | solution.py:264
  117.3 41.3 %turned_gram.1 = f32[32,144,1152]{2,1,0:T(8,128)} custom-call(s32[1]{0:T(128)} %bitcast.which_ref, bf16[4,8,9,96,128]{4,3,2,1,0:T(8,128)(2,1)} %exchange.1.buf_ref), custom_call_target="tpu_custom_call" | custom-call | tf_op jit(solution)/shard_map/turned_gram/pallas_call | solution.py:337
Async XLA Ops:
  4.3 1.8 %copy-start = (bf16[72,2,48,128]{3,2,1,0:T(8,128)(2,1)}, bf16[72,2,48,128]{3,2,1,0:T(8,128)(2,1)S(1)}, u32[]{:S(2)}) copy-start(bf16[72,2,48,128]{3,2,1,0:T(8,128)(2,1)S(1)} %reshape.9.own_ref) | copy-start | bytes 5308420
  4.3 3.6 %copy-start.3 = (s32[16,256]{1,0:T(8,128)S(1)}, s32[16,256]{1,0:T(8,128)}, u32[]{:S(2)}) copy-start(s32[16,256]{1,0:T(8,128)} %param.7) | copy-start | bytes 49156
  6.1 28.2 %collective-permute-start.1 = (bf16[72,2,32,128]{3,2,1,0:T(8,128)(2,1)}, bf16[72,2,32,128]{3,2,1,0:T(8,128)(2,1)S(1)}, u32[]{:S(2)}, u32[]{:S(2)}) collective-permute-start(bf16[72,2,32,128]{3,2,1,0:T(8,128)(2,1)} %get-tuple-element.5), channel_id=1, source_target_pairs={{1,0},{2,1},{3,2},{0,3},{5,4},{6,5},{7,6},{4,7},{9,8},{10,9},{11,1... | collective-permute-start | bytes 3538952 | tf_op jit(solution)/shard_map/ppermute | solution.py:125
  6.7 27.5 %collective-permute-start = (bf16[72,2,32,128]{3,2,1,0:T(8,128)(2,1)S(1)}, bf16[72,2,32,128]{3,2,1,0:T(8,128)(2,1)S(1)}, u32[]{:S(2)}, u32[]{:S(2)}) collective-permute-start(bf16[72,2,32,128]{3,2,1,0:T(8,128)(2,1)S(1)} %get-tuple-element.6), channel_id=1, source_target_pairs={{0,1},{1,2},{2,3},{3,0},{4,5},{5,6},{6,7},{7,4},{8,9},{9,10},{10,1... | collective-permute-start | bytes 3538952 | tf_op jit(solution)/shard_map/ppermute | solution.py:124
  34.2 1.1 copy-start.1
  34.2 1.5 copy-start.2

commit v3 on v2

--- a/solution.py
+++ b/solution.py
@@ -176,6 +176,19 @@
     )(which, gathered)
 
 
+def send_order(groups):
+    half = groups // 2
+    outer = sorted(range(half, groups), key=lambda o: (-(o // (half // 2 or 1)), o))
+    inner = list(range(2, half))
+    order = [o for o in (1,) if o < half]
+    while outer or inner:
+        if outer:
+            order.append(outer.pop(0))
+        if inner:
+            order.append(inner.pop(0))
+    return order
+
+
 def exchange_kernel(sent_ref, out_ref, own_sem, turn_send, turn_recv, far_send, far_recv, near_send, near_recv, pass_send, pass_recv):
     groups, peers = lax.axis_size("inp"), lax.axis_size("tm")
     chips = peers // CORES
@@ -189,6 +202,10 @@
     def back(step):
         return ((y + chips - step) % chips) * CORES + core
 
+    def pair(o):
+        bits = [(b, (g // b) % 2) for b in (1 << k for k in range(groups.bit_length() - 1))]
+        return sum(b * (1 - bit) if o & b else b * bit for b, bit in bits)
+
     def remote(src, dst, send, recv, to_g, to_t):
         return pltpu.make_async_remote_copy(
             src_ref=src, dst_ref=dst, send_sem=send, recv_sem=recv,
@@ -197,18 +214,18 @@
 
     barrier = pltpu.get_barrier_semaphore()
     for o in range(1, groups):
-        pl.semaphore_signal(barrier, inc=1, device_id={"inp": (g + o) % groups, "tm": t}, device_id_type=pl.DeviceIdType.MESH)
+        pl.semaphore_signal(barrier, inc=1, device_id={"inp": pair(o), "tm": t}, device_id_type=pl.DeviceIdType.MESH)
     for step in range(1, chips):
         pl.semaphore_signal(barrier, inc=1, device_id={"inp": g, "tm": far(step)}, device_id_type=pl.DeviceIdType.MESH)
     pl.semaphore_signal(barrier, inc=1, device_id={"inp": g, "tm": partner}, device_id_type=pl.DeviceIdType.MESH)
     pl.semaphore_wait(barrier, groups - 1 + chips - 1 + 1)
 
     def turn(o):
-        to = (g + o) % groups
+        to = pair(o)
         return remote(sent_ref.at[to], out_ref.at[t, g], turn_send.at[o], turn_recv.at[o], to, t)
 
     def slot(o):
-        return out_ref.at[t, (g + groups - o) % groups]
+        return out_ref.at[t, pair(o)]
 
     def spread(o, src):
         dst = slot(o)
@@ -216,10 +233,10 @@
         return copies + [remote(src, dst, near_send.at[o], near_recv.at[o], g, partner)]
 
     def relay(step, o):
-        piece = out_ref.at[back(step), (g + groups - o) % groups]
+        piece = out_ref.at[back(step), pair(o)]
         return remote(piece, piece, pass_send.at[step, o], pass_recv.at[step, o], g, partner)
 
-    order = list(range(1, groups))
+    order = send_order(groups)
     for o in order:
         turn(o).start()
     own = pltpu.make_async_copy(sent_ref.at[g], out_ref.at[t, g], own_sem)
@@ -229,18 +246,20 @@
 
     def land(o):
         for step in range(1, chips):
-            piece = out_ref.at[back(step), (g + groups - o) % groups]
+            piece = out_ref.at[back(step), pair(o)]
             remote(piece, piece, far_send.at[step, o], far_recv.at[step, o], g, far(step)).wait_recv()
             relay(step, o).start()
 
-    previous = 0
+    pending = [0]
     for o in order:
         turn(o).wait_recv()
         for copy in spread(o, slot(o)):
             copy.start()
-        land(previous)
-        previous = o
-    land(previous)
+        pending.append(o)
+        if len(pending) > 2:
+            land(pending.pop(0))
+    for o in pending:
+        land(o)
     own.wait()
     for o in range(groups):
         if o:
@@ -248,12 +267,12 @@
         src = slot(o) if o else sent_ref.at[g]
         for copy in spread(o, src):
             copy.wait_send()
-        piece = out_ref.at[partner, (g + groups - o) % groups]
+        piece = out_ref.at[partner, pair(o)]
         remote(piece, piece, near_send.at[o], near_recv.at[o], g, partner).wait_recv()
         for step in range(1, chips):
             relay(step, o).wait_send()
             other = ((y + chips - step) % chips) * CORES + (CORES - 1 - core)
-            piece = out_ref.at[other, (g + groups - o) % groups]
+            piece = out_ref.at[other, pair(o)]
             remote(piece, piece, pass_send.at[step, o], pass_recv.at[step, o], g, partner).wait_recv()
 
 
@@ -276,56 +295,64 @@
 
 
 def turned_gram_kernel(scale, channels, which_ref, buf_ref, out_ref, lined, mine):
-    peers, groups, steps, rows, _ = buf_ref.shape
+    _, groups, steps, rows, _ = buf_ref.shape
     inputs = groups * steps * GROUP
     width = 2 * channels
     packs = LANES // width
     depth = lined.shape[1] // channels
     half = depth // 2
-    spectra = half // peers
-    per_pack = spectra // packs
-    tiles = lined.shape[0]
-    height = out_ref.shape[1]
-    f = pl.program_id(0)
-
-    @pl.when(f == 0)
+    per_pack = rows // GROUP
+    spectra = per_pack * packs
+    peers = half // spectra
+    some, height = out_ref.shape[0], out_ref.shape[1]
+    taken = height // (steps * GROUP)
+    i = pl.program_id(0)
+
+    @pl.when(i < peers)
     def _():
-        @pl.loop(0, peers * (rows // 16))
-        def _(index):
-            t, pair = index // (rows // 16), index % (rows // 16)
-            block = buf_ref[t, :, :, pl.ds(pl.multiple_of(pair * 16, 16), 16), :].astype(jnp.float32)
-            block = block.reshape(groups * steps, 2, GROUP, LANES)
-            for u in range(2):
-                value = block[:, u].reshape(inputs, LANES)
-                for a in range(tiles):
-                    count = min(LANES, inputs - a * LANES)
-                    moved = value[a * LANES : a * LANES + count].T
-                    for j in range(packs):
-                        for d in range(2):
-                            line = d * half + t * spectra + j * per_pack + pair * 2 + u
-                            first = j * width + d * channels
-                            piece = moved[first : first + channels]
-                            if count == LANES:
-                                lined[a, pl.ds(line, channels, stride=depth), :] = piece
-                            else:
-                                lined[a, pl.ds(line, channels, stride=depth), :] = jnp.concatenate(
-                                    [piece, jnp.zeros((channels, LANES - count), jnp.float32)], axis=1
-                                )
-
-    start = pl.multiple_of(f * depth, 8)
-    x = jnp.concatenate([lined[a, pl.ds(start, depth), :] for a in range(tiles)], axis=1)
-    for t in range(inputs // height):
-
-        @pl.when(which_ref[0] == t)
-        def _():
-            mine[...] = x[:, t * height : (t + 1) * height]
-
-    left = mine[...]
-    other = jnp.concatenate([left[half:], -left[:half]], axis=0)
-    both = jnp.concatenate([left.T, other.T], axis=0).astype(jnp.bfloat16)
-    result = jnp.dot(both, x.astype(jnp.bfloat16), preferred_element_type=jnp.float32) * scale
-    out_ref[0, :, 0:inputs] = result[:height, :inputs]
-    out_ref[0, :, inputs : 2 * inputs] = result[height:, :inputs]
+        @pl.loop(0, rows // 16)
+        def _(pair):
+            span = pl.ds(pl.multiple_of(pair * 16, 16), 16)
+            for kept, block in ((lined, buf_ref[0, :, :, span, :]), (mine, buf_ref[0, pl.ds(which_ref[0] * taken, taken), :, span, :])):
+                block = block.astype(jnp.float32)
+                block = block.reshape(block.shape[0] * steps, 2, GROUP, LANES)
+                for u in range(2):
+                    value = block[:, u].reshape(block.shape[0] * GROUP, LANES)
+                    for a in range(kept.shape[0]):
+                        moved = value[a * LANES : (a + 1) * LANES].T
+                        count = moved.shape[1]
+                        if count < LANES:
+                            moved = jnp.concatenate([moved, jnp.zeros((LANES, LANES - count), jnp.float32)], axis=1)
+                        for j in range(packs):
+                            for d in range(2):
+                                line = d * half + i * spectra + j * per_pack + pair * 2 + u
+                                first = j * width + d * channels
+                                kept[a, pl.ds(line, channels, stride=depth), :] = moved[first : first + channels]
+
+    room = -(-half // LANES) * LANES
+    blank = room - half
+
+    def parts(kept, start):
+        return [
+            jnp.concatenate([kept[a, pl.ds(start + d * half, half), :] for a in range(kept.shape[0])], axis=1)
+            for d in range(2)
+        ]
+
+    def filled(value):
+        if not blank:
+            return value
+        return jnp.concatenate([value, jnp.zeros((blank, value.shape[1]), value.dtype)], axis=0)
+
+    @pl.when(i >= peers)
+    def _():
+        for k in range(some):
+            start = pl.multiple_of(((i - peers) * some + k) * depth, 8)
+            x = jnp.concatenate([filled(v.astype(jnp.bfloat16)) for v in parts(lined, start)], axis=0)
+            re, im = [filled(v).T[:height] for v in parts(mine, start)]
+            both = jnp.concatenate([jnp.concatenate([re, im], axis=1), jnp.concatenate([im, -re], axis=1)], axis=0)
+            result = jnp.dot(both.astype(jnp.bfloat16), x, preferred_element_type=jnp.float32) * scale
+            out_ref[k, :, 0:inputs] = result[:height, :inputs]
+            out_ref[k, :, inputs : 2 * inputs] = result[height:, :inputs]
 
 
 def turned_gram(buf, channels, height, scale):
@@ -333,18 +360,19 @@
     inputs = groups * steps * GROUP
     packs = LANES // (2 * channels)
     depth = 2 * peers * packs * rows // GROUP
+    some = math.gcd(channels, 4)
     which = lax.axis_index("tm").astype(jnp.int32).reshape(1)
     return pl.pallas_call(
         functools.partial(turned_gram_kernel, scale, channels),
         out_shape=jax.ShapeDtypeStruct((channels, height, 2 * inputs), jnp.float32),
         grid_spec=pltpu.PrefetchScalarGridSpec(
             num_scalar_prefetch=1,
-            grid=(channels,),
-            in_specs=[pl.BlockSpec(buf.shape, lambda f, w: (0, 0, 0, 0, 0), pipeline_mode=pl.Buffered(1))],
-            out_specs=pl.BlockSpec((1, height, 2 * inputs), lambda f, w: (f, 0, 0)),
+            grid=(peers + channels // some,),
+            in_specs=[pl.BlockSpec((1, groups, steps, rows, LANES), lambda i, w: (jnp.minimum(i, peers - 1), 0, 0, 0, 0))],
+            out_specs=pl.BlockSpec((some, height, 2 * inputs), lambda i, w: (jnp.maximum(i - peers, 0), 0, 0)),
             scratch_shapes=[
                 pltpu.VMEM((-(-inputs // LANES), channels * depth, LANES), jnp.float32),
-                pltpu.VMEM((depth, height), jnp.float32),
+                pltpu.VMEM((-(-height // LANES), channels * depth, LANES), jnp.float32),
             ],
         ),
         name="turned_gram",
@@ -360,7 +388,8 @@
     mine = channels // groups
     packs = LANES // (2 * mine)
     sent = front(samples, delays, taps)
-    if local_inputs % GROUP == 0 and sent.shape[2] % 16 == 0:
+    direct = local_inputs % GROUP == 0 and sent.shape[2] % 16 == 0 and groups & (groups - 1) == 0
+    if direct and (inputs // peers) % local_inputs == 0:
         return turned_gram(exchange(sent), mine, inputs // peers, 1.0 / (spectra * peers))
     turned = lax.all_to_all(sent, "inp", split_axis=0, concat_axis=0, tiled=True)
     steps = turned.shape[1]

time: 159 us -> 141 us (0.89)
  the two profiles are of different devices: /device:TPU:25 before, /device:TPU:11 now
where the time goes in v3:
time: 141 us
  Pallas kernels  105 us (74%)
  waiting for transfers between devices  25 us (18%)
  local copies, waits for them, and re-layouts  8.25 us (6%)
  starting transfers between devices  1.8 us (1%)
    pallas_call x1, Pallas kernels, exchange(): pl.pallas_call(exchange_kernel, out_shape=jax.ShapeDtypeStruct((peers,) +...  60 us
    pallas_call x1, Pallas kernels, turned_gram(): pl.pallas_call(functools.partial(turned_gram_kernel, scale, channels), ou...  30.7 us
    ppermute x1, waiting for transfers between devices, front(): after = lax.ppermute(lined[:, :, :hist], 'tm', down)  25 us
    pallas_call x1, Pallas kernels, front(): pl.pallas_call(functools.partial(spectra_kernel, (tap_count, parts, spect...  14.8 us
    reshape x1, local copies, waits for them, and re-layouts, front(): lined = samples.reshape(local_inputs, 2, own, LANES)  4.29 us
  transfers between devices with their start and end apart: 2, of which 1 were waited for; matrix products, arithmetic and copies ran while one was open for 1% of the time, Pallas kernels for 0%

profile of v3, /device:TPU:11, one launch (start us, length us, event | category | flops | bytes accessed | tf_op | source)
XLA Modules:
  0.0 141.2 jit_solution(2905416181819032205)
XLA Ops:
  0.0 4.3 %reshape.9.own_ref = bf16[72,2,48,128]{3,2,1,0:T(8,128)(2,1)S(1)} reshape(bf16[72,2,6144]{2,1,0:T(2,128)(2,1)} %param.5) | data formatting | bytes 3538944 | tf_op jit(solution)/shard_map/reshape | solution.py:121
  4.3 0.0 copy-start
  4.3 0.0 copy-start.3
  4.3 1.7 %fusion = (bf16[72,2,32,128]{3,2,1,0:T(8,128)(2,1)}, bf16[72,2,32,128]{3,2,1,0:T(8,128)(2,1)S(1)}) fusion(bf16[72,2,48,128]{3,2,1,0:T(8,128)(2,1)S(1)} %reshape.9.own_ref), kind=kLoop, calls=%fused_computation.1 | loop fusion | bytes 4718592 | tf_op jit(solution)/shard_map/slice | solution.py:125
  6.1 0.0 copy-done
  6.1 0.7 collective-permute-start.1
  6.7 1.1 collective-permute-start
  7.9 0.0 copy-done.3
  7.9 0.6 convert_multiply_fusion
  8.5 0.7 broadcast_in_dim.7
  9.2 25.0 %collective-permute-done.1.after_ref = bf16[72,2,32,128]{3,2,1,0:T(8,128)(2,1)S(1)} collective-permute-done((bf16[72,2,32,128]{3,2,1,0:T(8,128)(2,1)}, bf16[72,2,32,128]{3,2,1,0:T(8,128)(2,1)S(1)}, u32[]{:S(2)}, u32[]{:S(2)}) %collective-permute-start.1) | collective-permute-done | bytes 1179680 | tf_op jit(solution)/shard_map/ppermute | solution.py:125
  34.2 0.0 copy-start.1
  34.2 0.0 collective-permute-done.before_ref
  34.2 0.0 copy-start.2
  34.2 0.7 broadcast_in_dim.8.coef_ref
  35.0 0.3 copy-done.1
  35.3 0.4 copy-done.2
  35.7 14.8 %spectra.1.sent_ref = bf16[8,9,96,128]{3,2,1,0:T(8,128)(2,1)} custom-call(s32[72]{0:T(128)} %delays_ref.1, bf16[72,2,32,128]{3,2,1,0:T(8,128)(2,1)} %copy-done.2, bf16[72,2,48,128]{3,2,1,0:T(8,128)(2,1)} %copy-done, bf16[72,2,32,128]{3,2,1,0:T(8,128)(2,1)} %copy-done.1, f32[16,2,8,128]{3,2,1,0:T(8,128)} %broadcast_in_dim.8.coef_ref, ...), custom_call_target="tpu_custom_call" | custom-call | tf_op jit(solution)/shard_map/spectra/pallas_call | solution.py:137
  50.5 60.0 %exchange.1.buf_ref = bf16[4,8,9,96,128]{4,3,2,1,0:T(8,128)(2,1)} custom-call(bf16[8,9,96,128]{3,2,1,0:T(8,128)(2,1)} %spectra.1.sent_ref), custom_call_target="tpu_custom_call" | custom-call | tf_op jit(solution)/shard_map/exchange/pallas_call | solution.py:283
  110.5 30.7 %turned_gram.1 = f32[32,144,1152]{2,1,0:T(8,128)} custom-call(s32[1]{0:T(128)} %bitcast.which_ref, bf16[4,8,9,96,128]{4,3,2,1,0:T(8,128)(2,1)} %exchange.1.buf_ref), custom_call_target="tpu_custom_call" | custom-call | tf_op jit(solution)/shard_map/turned_gram/pallas_call | solution.py:365
Async XLA Ops:
  4.3 1.8 %copy-start = (bf16[72,2,48,128]{3,2,1,0:T(8,128)(2,1)}, bf16[72,2,48,128]{3,2,1,0:T(8,128)(2,1)S(1)}, u32[]{:S(2)}) copy-start(bf16[72,2,48,128]{3,2,1,0:T(8,128)(2,1)S(1)} %reshape.9.own_ref) | copy-start | bytes 5308420
  4.3 3.6 %copy-start.3 = (s32[16,256]{1,0:T(8,128)S(1)}, s32[16,256]{1,0:T(8,128)}, u32[]{:S(2)}) copy-start(s32[16,256]{1,0:T(8,128)} %param.7) | copy-start | bytes 49156
  6.1 28.2 %collective-permute-start.1 = (bf16[72,2,32,128]{3,2,1,0:T(8,128)(2,1)}, bf16[72,2,32,128]{3,2,1,0:T(8,128)(2,1)S(1)}, u32[]{:S(2)}, u32[]{:S(2)}) collective-permute-start(bf16[72,2,32,128]{3,2,1,0:T(8,128)(2,1)} %get-tuple-element.5), channel_id=1, source_target_pairs={{1,0},{2,1},{3,2},{0,3},{5,4},{6,5},{7,6},{4,7},{9,8},{10,9},{11,1... | collective-permute-start | bytes 3538952 | tf_op jit(solution)/shard_map/ppermute | solution.py:125
  6.7 27.5 %collective-permute-start = (bf16[72,2,32,128]{3,2,1,0:T(8,128)(2,1)S(1)}, bf16[72,2,32,128]{3,2,1,0:T(8,128)(2,1)S(1)}, u32[]{:S(2)}, u32[]{:S(2)}) collective-permute-start(bf16[72,2,32,128]{3,2,1,0:T(8,128)(2,1)S(1)} %get-tuple-element.6), channel_id=1, source_target_pairs={{0,1},{1,2},{2,3},{3,0},{4,5},{5,6},{6,7},{7,4},{8,9},{9,10},{10,1... | collective-permute-start | bytes 3538952 | tf_op jit(solution)/shard_map/ppermute | solution.py:124
  34.2 1.1 copy-start.1
  34.2 1.5 %copy-start.2 = (bf16[72,2,32,128]{3,2,1,0:T(8,128)(2,1)}, bf16[72,2,32,128]{3,2,1,0:T(8,128)(2,1)S(1)}, u32[]{:S(2)}) copy-start(bf16[72,2,32,128]{3,2,1,0:T(8,128)(2,1)S(1)} %collective-permute-done.before_ref) | copy-start | bytes 3538948

commit v4 on v3

--- a/solution.py
+++ b/solution.py
@@ -12,6 +12,7 @@
 LANES = 128
 GROUP = 8
 CORES = 2
+CHUNKS = 3
 
 
 def dft_tables(length, groups):
@@ -26,13 +27,14 @@
     return high, low
 
 
-def spectra_kernel(dims, delays_ref, before_ref, own_ref, after_ref, coef_ref, high_ref, low_ref, out_ref, flat, slab, filt):
-    tap_count, parts, spectra, hist, skip = dims
+def spectra_kernel(dims, delays_ref, before_ref, own_ref, after_ref, coef_ref, high_ref, low_ref, *rest):
+    out_ref, flat, slab, filt = rest[-4:]
+    tap_count, parts, spectra, hist, skip, base = dims
     own = own_ref.shape[2]
     groups = out_ref.shape[0]
     frames = spectra + tap_count - 1
     need = -(-frames * parts // GROUP) * GROUP
-    step = pl.program_id(0)
+    step = pl.program_id(0) + base
     lane = lax.broadcasted_iota(jnp.int32, (need, LANES), 1)
     for c in range(2):
         for j in range(GROUP):
@@ -118,12 +120,18 @@
     margin_rows = (tap_count - 1) * parts
     hist = -(-margin_rows // 16) * 16
     own = shard_len // LANES
-    lined = samples.reshape(local_inputs, 2, own, LANES)
     up = [(i, (i + 1) % peers) for i in range(peers)]
     down = [(j, i) for i, j in up]
-    before = lax.ppermute(lined[:, :, own - hist :], "tm", up)
-    after = lax.ppermute(lined[:, :, :hist], "tm", down)
     steps = -(-local_inputs // GROUP)
+    chunks = CHUNKS if local_inputs % (GROUP * CHUNKS) == 0 else 1
+    span = local_inputs // chunks
+    halos = []
+    for k in range(chunks):
+        piece = samples[k * span : (k + 1) * span]
+        tail = piece[:, :, shard_len - hist * LANES :].reshape(span, 2, hist, LANES)
+        head = piece[:, :, : hist * LANES].reshape(span, 2, hist, LANES)
+        halos.append((lax.ppermute(tail, "tm", up), lax.ppermute(head, "tm", down)))
+    lined = samples.reshape(local_inputs, 2, own, LANES)
     offsets = jnp.pad(delays, (0, steps * GROUP - local_inputs))
     coef = (taps.astype(jnp.float32) * (1.0 / 4096.0)).reshape(tap_count, parts, 1, LANES)
     coef = jnp.broadcast_to(coef, (tap_count, parts, GROUP, LANES))
@@ -134,29 +142,44 @@
     need = -(-(spectra + tap_count - 1) * parts // GROUP) * GROUP
     total = -(-max(2 * hist + own, need + hist + 1) // GROUP) * GROUP
     fixed = lambda shape: pl.BlockSpec(shape, lambda i, d: (0,) * len(shape))
-    return pl.pallas_call(
-        functools.partial(spectra_kernel, (tap_count, parts, spectra, hist, hist - margin_rows)),
-        out_shape=jax.ShapeDtypeStruct((groups, steps, rows, LANES), jnp.bfloat16),
-        grid_spec=pltpu.PrefetchScalarGridSpec(
-            num_scalar_prefetch=1,
-            grid=(steps,),
-            in_specs=[
-                pl.BlockSpec((GROUP, 2, hist, LANES), lambda i, d: (i, 0, 0, 0)),
-                pl.BlockSpec((GROUP, 2, own, LANES), lambda i, d: (i, 0, 0, 0)),
-                pl.BlockSpec((GROUP, 2, hist, LANES), lambda i, d: (i, 0, 0, 0)),
-                fixed(coef.shape),
-                fixed(high.shape),
-                fixed(low.shape),
-            ],
-            out_specs=pl.BlockSpec((groups, 1, rows, LANES), lambda i, d: (0, i, 0, 0)),
-            scratch_shapes=[
-                pltpu.VMEM((4, total, LANES), jnp.float32),
-                pltpu.VMEM((2, need * GROUP, LANES), jnp.float32),
-                pltpu.VMEM((spectra * GROUP, 2 * channels), jnp.float32),
-            ],
-        ),
-        name="spectra",
-    )(offsets, before, lined, after, coef, jnp.asarray(high), jnp.asarray(low))
+    sent = None
+    for k in range(chunks):
+        base, count = k * steps // chunks, steps // chunks
+        before, after = halos[k]
+        operands = [offsets, before, lined, after, coef, jnp.asarray(high), jnp.asarray(low)]
+        in_specs = [
+            pl.BlockSpec((GROUP, 2, hist, LANES), lambda i, d: (i, 0, 0, 0)),
+            pl.BlockSpec((GROUP, 2, own, LANES), lambda i, d, base=base: (i + base, 0, 0, 0)),
+            pl.BlockSpec((GROUP, 2, hist, LANES), lambda i, d: (i, 0, 0, 0)),
+            fixed(coef.shape),
+            fixed(high.shape),
+            fixed(low.shape),
+        ]
+        aliases = {}
+        if sent is not None:
+            aliases = {len(operands): 0}
+            operands.append(sent)
+            in_specs.append(pl.BlockSpec(memory_space=pl.ANY))
+        flops = 6 * count * GROUP * spectra * (2 * channels) ** 2
+        sent = pl.pallas_call(
+            functools.partial(spectra_kernel, (tap_count, parts, spectra, hist, hist - margin_rows, base)),
+            out_shape=jax.ShapeDtypeStruct((groups, steps, rows, LANES), jnp.bfloat16),
+            grid_spec=pltpu.PrefetchScalarGridSpec(
+                num_scalar_prefetch=1,
+                grid=(count,),
+                in_specs=in_specs,
+                out_specs=pl.BlockSpec((groups, 1, rows, LANES), lambda i, d, base=base: (0, i + base, 0, 0)),
+                scratch_shapes=[
+                    pltpu.VMEM((4, total, LANES), jnp.float32),
+                    pltpu.VMEM((2, need * GROUP, LANES), jnp.float32),
+                    pltpu.VMEM((spectra * GROUP, 2 * channels), jnp.float32),
+                ],
+            ),
+            input_output_aliases=aliases,
+            cost_estimate=pl.CostEstimate(flops=flops, bytes_accessed=16 << 20, transcendentals=0),
+            name="spectra",
+        )(*operands)
+    return sent
 
 
 def gram(gathered, rows, scale):

time: 141 us -> 136 us (0.965)
  waiting for transfers between devices: 25 us -> 3.16 us
  local copies, waits for them, and re-layouts: 8.25 us -> 16.9 us
  Pallas kernels: 105 us -> 110 us
  starting transfers between devices: 1.8 us -> 5.35 us
    ppermute x2 -> x6, waiting for transfers between devices: 25 us -> 3.16 us  [front(): halos.append((lax.ppermute(tail, 'tm', up), lax.ppermute(head, 'tm', down)))]
    reshape x0 -> x6, local copies, waits for them, and re-layouts: none -> 6.51 us  [the longest x3 3.37 us: front(): head = piece[:, :, :hist * LANES].reshape(span, 2, hist, LANES)]
    pallas_call x1 -> x3, Pallas kernels: 14.8 us -> 20.5 us  [front(): pl.pallas_call(functools.partial(spectra_kernel, (tap_count, parts, spect...]
    ppermute x2 -> x6, starting transfers between devices: 1.8 us -> 5.35 us  [front(): halos.append((lax.ppermute(tail, 'tm', up), lax.ppermute(head, 'tm', down)))]
    slice x1, local copies, waits for them, and re-layouts: 1.74 us -> 5.12 us  [front(): head = piece[:, :, :hist * LANES].reshape(span, 2, hist, LANES)]
    reshape x1, local copies, waits for them, and re-layouts: 4.29 us -> 2.37 us  [front(): lined = samples.reshape(local_inputs, 2, own, LANES)]
    unnamed x8 -> x12, local copies, waits for them, and re-layouts: 0.76 us -> 2.22 us
  transfers between devices with their start and end apart: 2 -> 6, of which waited for: 1 -> 2; matrix products, arithmetic and copies ran while one was open for 1% -> 6% of each run, Pallas kernels for 0% -> 10%
where the time goes in v4:
time: 136 us
  Pallas kernels  110 us (81%)
  local copies, waits for them, and re-layouts  16.9 us (12%)
  starting transfers between devices  5.35 us (4%)
  waiting for transfers between devices  3.16 us (2%)
    pallas_call x1, Pallas kernels, exchange(): pl.pallas_call(exchange_kernel, out_shape=jax.ShapeDtypeStruct((peers,) +...  58.9 us
    pallas_call x1, Pallas kernels, turned_gram(): pl.pallas_call(functools.partial(turned_gram_kernel, scale, channels), ou...  30.7 us
    pallas_call x3, Pallas kernels, front(): pl.pallas_call(functools.partial(spectra_kernel, (tap_count, parts, spect...  20.5 us
    ppermute x6, starting transfers between devices, front(): halos.append((lax.ppermute(tail, 'tm', up), lax.ppermute(head, 'tm', down)))  5.35 us
    slice x1, local copies, waits for them, and re-layouts, front(): head = piece[:, :, :hist * LANES].reshape(span, 2, hist, LANES)  5.12 us
    reshape x3, local copies, waits for them, and re-layouts, front(): head = piece[:, :, :hist * LANES].reshape(span, 2, hist, LANES)  3.37 us
    ppermute x6, waiting for transfers between devices, front(): halos.append((lax.ppermute(tail, 'tm', up), lax.ppermute(head, 'tm', down)))  3.16 us
    reshape x3, local copies, waits for them, and re-layouts, front(): tail = piece[:, :, shard_len - hist * LANES:].reshape(span, 2, hist, LANES)  3.14 us
  transfers between devices with their start and end apart: 6, of which 2 were waited for; matrix products, arithmetic and copies ran while one was open for 6% of the time, Pallas kernels for 10%

profile of v4, /device:TPU:11, one launch (start us, length us, event | category | flops | bytes accessed | tf_op | source)
XLA Modules:
  0.0 135.6 jit_solution(5211206844530500568)
XLA Ops:
  0.0 5.1 %fusion = (bf16[24,2,4096]{2,1,0:T(2,128)(2,1)}, bf16[24,2,4096]{2,1,0:T(2,128)(2,1)S(1)}, bf16[24,2,4096]{2,1,0:T(2,128)(2,1)S(1)}, bf16[24,2,4096]{2,1,0:T(2,1...) fusion(bf16[72,2,6144]{2,1,0:T(2,128)(2,1)} %param.5), kind=kLoop, calls=%fused_computation.1 | loop fusion | bytes 4718592 | tf_op jit(solution)/shard_map/slice | solution.py:132
  5.1 1.0 reshape.32
  6.2 1.8 %collective-permute-start.4 = (bf16[24,2,32,128]{3,2,1,0:T(8,128)(2,1)}, bf16[24,2,32,128]{3,2,1,0:T(8,128)(2,1)}, u32[]{:S(2)}, u32[]{:S(2)}) collective-permute-start(bf16[24,2,32,128]{3,2,1,0:T(8,128)(2,1)} %reshape.32), channel_id=1, source_target_pairs={{0,1},{1,2},{2,3},{3,0},{4,5},{5,6},{6,7},{7,4},{8,9},{9,10},{10,1... | collective-permute-start | bytes 1179656 | tf_op jit(solution)/shard_map/ppermute | solution.py:133
  8.0 2.0 %reshape.33 = bf16[24,2,32,128]{3,2,1,0:T(8,128)(2,1)} reshape(bf16[24,2,4096]{2,1,0:T(2,128)(2,1)} %get-tuple-element.5) | data formatting | bytes 786432 | tf_op jit(solution)/shard_map/reshape | solution.py:132
  10.0 1.1 reshape.30
  11.1 1.7 %collective-permute-start.2 = (bf16[24,2,32,128]{3,2,1,0:T(8,128)(2,1)}, bf16[24,2,32,128]{3,2,1,0:T(8,128)(2,1)S(1)}, u32[]{:S(2)}, u32[]{:S(2)}) collective-permute-start(bf16[24,2,32,128]{3,2,1,0:T(8,128)(2,1)} %reshape.30), channel_id=1, source_target_pairs={{0,1},{1,2},{2,3},{3,0},{4,5},{5,6},{6,7},{7,4},{8,9},{9,10},{10,1... | collective-permute-start | bytes 1179656 | tf_op jit(solution)/shard_map/ppermute | solution.py:133
  12.8 1.0 reshape.31
  13.8 1.0 reshape.27
  14.9 1.7 %collective-permute-start = (bf16[24,2,32,128]{3,2,1,0:T(8,128)(2,1)}, bf16[24,2,32,128]{3,2,1,0:T(8,128)(2,1)S(1)}, u32[]{:S(2)}, u32[]{:S(2)}) collective-permute-start(bf16[24,2,32,128]{3,2,1,0:T(8,128)(2,1)} %reshape.27), channel_id=1, source_target_pairs={{0,1},{1,2},{2,3},{3,0},{4,5},{5,6},{6,7},{7,4},{8,9},{9,10},{10,1... | collective-permute-start | bytes 1179656 | tf_op jit(solution)/shard_map/ppermute | solution.py:133
  16.6 2.4 %reshape.28.own_ref = bf16[72,2,48,128]{3,2,1,0:T(8,128)(2,1)} reshape(bf16[72,2,6144]{2,1,0:T(2,128)(2,1)S(1)} %copy-done) | data formatting | bytes 3538944 | tf_op jit(solution)/shard_map/reshape | solution.py:134
  19.0 0.3 reshape.29
  19.3 0.0 collective-permute-done.4.before_ref
  19.3 0.1 collective-permute-start.1
  19.4 2.2 %collective-permute-done.5.after_ref = bf16[24,2,32,128]{3,2,1,0:T(8,128)(2,1)} collective-permute-done((bf16[24,2,32,128]{3,2,1,0:T(8,128)(2,1)}, bf16[24,2,32,128]{3,2,1,0:T(8,128)(2,1)}, u32[]{:S(2)}, u32[]{:S(2)}) %collective-permute-start.5) | collective-permute-done | bytes 393248 | tf_op jit(solution)/shard_map/ppermute | solution.py:133
  21.6 0.7 broadcast_in_dim.8.coef_ref
  22.3 6.8 %spectra.3.rest_0_ = bf16[8,9,96,128]{3,2,1,0:T(8,128)(2,1)} custom-call(s32[72]{0:T(128)} %delays_ref.5, bf16[24,2,32,128]{3,2,1,0:T(8,128)(2,1)} %collective-permute-done.4.before_ref, bf16[72,2,48,128]{3,2,1,0:T(8,128)(2,1)} %reshape.28.own_ref, bf16[24,2,32,128]{3,2,1,0:T(8,128)(2,1)} %collective-permute-done.5.after_ref, ...), custom_call_target="tpu_custom_call" | custom-call | flops 905969664 | bytes 16777216 | tf_op jit(solution)/shard_map/spectra/pallas_call | solution.py:164
  29.1 0.9 collective-permute-done.3.after_ref
  30.1 0.7 copy-done.3
  30.8 6.8 %spectra.4.rest_0_ = bf16[8,9,96,128]{3,2,1,0:T(8,128)(2,1)} custom-call(s32[72]{0:T(128)} %delays_ref.5, bf16[24,2,32,128]{3,2,1,0:T(8,128)(2,1)} %copy-done.2, bf16[72,2,48,128]{3,2,1,0:T(8,128)(2,1)} %reshape.28.own_ref, bf16[24,2,32,128]{3,2,1,0:T(8,128)(2,1)} %copy-done.3, ...), custom_call_target="tpu_custom_call", output_to_operand_aliasing={{}: (7, {})} | custom-call | flops 905969664 | bytes 16777216 | tf_op jit(solution)/shard_map/spectra/pallas_call | solution.py:164
  37.7 0.7 copy-done.1
  38.4 0.7 copy-done.4
  39.1 6.9 %spectra.5.sent_ref = bf16[8,9,96,128]{3,2,1,0:T(8,128)(2,1)} custom-call(s32[72]{0:T(128)} %delays_ref.5, bf16[24,2,32,128]{3,2,1,0:T(8,128)(2,1)} %copy-done.1, bf16[72,2,48,128]{3,2,1,0:T(8,128)(2,1)} %reshape.28.own_ref, bf16[24,2,32,128]{3,2,1,0:T(8,128)(2,1)} %copy-done.4, ...), custom_call_target="tpu_custom_call", output_to_operand_aliasing={{}: (7, {})} | custom-call | flops 905969664 | bytes 16777216 | tf_op jit(solution)/shard_map/spectra/pallas_call | solution.py:164
  46.0 58.9 %exchange.1.buf_ref = bf16[4,8,9,96,128]{4,3,2,1,0:T(8,128)(2,1)} custom-call(bf16[8,9,96,128]{3,2,1,0:T(8,128)(2,1)} %spectra.5.sent_ref), custom_call_target="tpu_custom_call" | custom-call | tf_op jit(solution)/shard_map/exchange/pallas_call | solution.py:306
  104.9 30.7 %turned_gram.1 = f32[32,144,1152]{2,1,0:T(8,128)} custom-call(s32[1]{0:T(128)} %bitcast.which_ref, bf16[4,8,9,96,128]{4,3,2,1,0:T(8,128)(2,1)} %exchange.1.buf_ref), custom_call_target="tpu_custom_call" | custom-call | tf_op jit(solution)/shard_map/turned_gram/pallas_call | solution.py:388
  (16 shorter events, 0.0 us)
Async XLA Ops:
  6.2 10.5 %copy-start = (bf16[72,2,6144]{2,1,0:T(2,128)(2,1)S(1)}, bf16[72,2,6144]{2,1,0:T(2,128)(2,1)}, u32[]{:S(2)}) copy-start(bf16[72,2,6144]{2,1,0:T(2,128)(2,1)} %param.5) | copy-start | bytes 5308420
  6.2 13.2 %collective-permute-start.4 = (bf16[24,2,32,128]{3,2,1,0:T(8,128)(2,1)}, bf16[24,2,32,128]{3,2,1,0:T(8,128)(2,1)}, u32[]{:S(2)}, u32[]{:S(2)}) collective-permute-start(bf16[24,2,32,128]{3,2,1,0:T(8,128)(2,1)} %reshape.32), channel_id=1, source_target_pairs={{0,1},{1,2},{2,3},{3,0},{4,5},{5,6},{6,7},{7,4},{8,9},{9,10},{10,1... | collective-permute-start | bytes 1179656 | tf_op jit(solution)/shard_map/ppermute | solution.py:133
  10.0 11.6 %collective-permute-start.5 = (bf16[24,2,32,128]{3,2,1,0:T(8,128)(2,1)}, bf16[24,2,32,128]{3,2,1,0:T(8,128)(2,1)}, u32[]{:S(2)}, u32[]{:S(2)}) collective-permute-start(bf16[24,2,32,128]{3,2,1,0:T(8,128)(2,1)} %reshape.33), channel_id=1, source_target_pairs={{1,0},{2,1},{3,2},{0,3},{5,4},{6,5},{7,6},{4,7},{9,8},{10,9},{11,1... | collective-permute-start | bytes 1179656 | tf_op jit(solution)/shard_map/ppermute | solution.py:133
  11.1 18.1 %collective-permute-start.2 = (bf16[24,2,32,128]{3,2,1,0:T(8,128)(2,1)}, bf16[24,2,32,128]{3,2,1,0:T(8,128)(2,1)S(1)}, u32[]{:S(2)}, u32[]{:S(2)}) collective-permute-start(bf16[24,2,32,128]{3,2,1,0:T(8,128)(2,1)} %reshape.30), channel_id=1, source_target_pairs={{0,1},{1,2},{2,3},{3,0},{4,5},{5,6},{6,7},{7,4},{8,9},{9,10},{10,1... | collective-permute-start | bytes 1179656 | tf_op jit(solution)/shard_map/ppermute | solution.py:133
  13.8 16.2 %collective-permute-start.3 = (bf16[24,2,32,128]{3,2,1,0:T(8,128)(2,1)}, bf16[24,2,32,128]{3,2,1,0:T(8,128)(2,1)S(1)}, u32[]{:S(2)}, u32[]{:S(2)}) collective-permute-start(bf16[24,2,32,128]{3,2,1,0:T(8,128)(2,1)} %reshape.31), channel_id=1, source_target_pairs={{1,0},{2,1},{3,2},{0,3},{5,4},{6,5},{7,6},{4,7},{9,8},{10,9},{11,1... | collective-permute-start | bytes 1179656 | tf_op jit(solution)/shard_map/ppermute | solution.py:133
  14.9 22.8 %collective-permute-start = (bf16[24,2,32,128]{3,2,1,0:T(8,128)(2,1)}, bf16[24,2,32,128]{3,2,1,0:T(8,128)(2,1)S(1)}, u32[]{:S(2)}, u32[]{:S(2)}) collective-permute-start(bf16[24,2,32,128]{3,2,1,0:T(8,128)(2,1)} %reshape.27), channel_id=1, source_target_pairs={{0,1},{1,2},{2,3},{3,0},{4,5},{5,6},{6,7},{7,4},{8,9},{9,10},{10,1... | collective-permute-start | bytes 1179656 | tf_op jit(solution)/shard_map/ppermute | solution.py:133
  16.6 2.8 %copy-start.5 = (s32[16,256]{1,0:T(8,128)S(1)}, s32[16,256]{1,0:T(8,128)}, u32[]{:S(2)}) copy-start(s32[16,256]{1,0:T(8,128)} %param.7) | copy-start | bytes 49156
  19.3 18.3 %collective-permute-start.1 = (bf16[24,2,32,128]{3,2,1,0:T(8,128)(2,1)S(1)}, bf16[24,2,32,128]{3,2,1,0:T(8,128)(2,1)S(1)}, u32[]{:S(2)}, u32[]{:S(2)}) collective-permute-start(bf16[24,2,32,128]{3,2,1,0:T(8,128)(2,1)S(1)} %reshape.29), channel_id=1, source_target_pairs={{1,0},{2,1},{3,2},{0,3},{5,4},{6,5},{7,6},{4,7},{9,8},{10,9},{11,1... | collective-permute-start | bytes 1179656 | tf_op jit(solution)/shard_map/ppermute | solution.py:133
  29.1 0.9 copy-start.2
  30.1 0.7 copy-start.3
  37.7 0.7 copy-start.1
  38.4 0.7 copy-start.4

commit v5 on v4

--- a/solution.py
+++ b/solution.py
@@ -125,13 +125,12 @@
     steps = -(-local_inputs // GROUP)
     chunks = CHUNKS if local_inputs % (GROUP * CHUNKS) == 0 else 1
     span = local_inputs // chunks
+    lined = samples.reshape(local_inputs, 2, own, LANES)
     halos = []
     for k in range(chunks):
-        piece = samples[k * span : (k + 1) * span]
-        tail = piece[:, :, shard_len - hist * LANES :].reshape(span, 2, hist, LANES)
-        head = piece[:, :, : hist * LANES].reshape(span, 2, hist, LANES)
+        piece = lined[k * span : (k + 1) * span]
+        tail, head = piece[:, :, own - hist :], piece[:, :, :hist]
         halos.append((lax.ppermute(tail, "tm", up), lax.ppermute(head, "tm", down)))
-    lined = samples.reshape(local_inputs, 2, own, LANES)
     offsets = jnp.pad(delays, (0, steps * GROUP - local_inputs))
     coef = (taps.astype(jnp.float32) * (1.0 / 4096.0)).reshape(tap_count, parts, 1, LANES)
     coef = jnp.broadcast_to(coef, (tap_count, parts, GROUP, LANES))

time: 136 us -> 132 us (0.971)
  local copies, waits for them, and re-layouts: 16.9 us -> 11.9 us
  Pallas kernels: 110 us -> 112 us
  starting transfers between devices: 5.35 us -> 3.55 us
    reshape x6 -> x0, local copies, waits for them, and re-layouts: 6.51 us -> none  [the longest x3 3.37 us: front(): head = piece[:, :, :hist * LANES].reshape(span, 2, hist, LANES)]
    pallas_call x1, Pallas kernels: 58.9 us -> 60.9 us  [exchange(): pl.pallas_call(exchange_kernel, out_shape=jax.ShapeDtypeStruct((peers,) +...]
    ppermute x6, starting transfers between devices: 5.35 us -> 3.55 us  [front(): halos.append((lax.ppermute(tail, 'tm', up), lax.ppermute(head, 'tm', down)))]
    slice x1 -> x7, local copies, waits for them, and re-layouts: 5.12 us -> 6.57 us  [the longest x4 3.75 us: front(): piece = lined[k * span:(k + 1) * span]]
  transfers between devices with their start and end apart: 6 -> 6, of which waited for: 2 -> 3; matrix products, arithmetic and copies ran while one was open for 6% -> 4% of each run, Pallas kernels for 10% -> 10%
where the time goes in v5:
time: 132 us
  Pallas kernels  112 us (85%)
  local copies, waits for them, and re-layouts  11.9 us (9%)
  waiting for transfers between devices  4.29 us (3%)
  starting transfers between devices  3.55 us (3%)
    pallas_call x1, Pallas kernels, exchange(): pl.pallas_call(exchange_kernel, out_shape=jax.ShapeDtypeStruct((peers,) +...  60.9 us
    pallas_call x1, Pallas kernels, turned_gram(): pl.pallas_call(functools.partial(turned_gram_kernel, scale, channels), ou...  30.7 us
    pallas_call x3, Pallas kernels, front(): pl.pallas_call(functools.partial(spectra_kernel, (tap_count, parts, spect...  20.5 us
    ppermute x6, waiting for transfers between devices, front(): halos.append((lax.ppermute(tail, 'tm', up), lax.ppermute(head, 'tm', down)))  4.29 us
    slice x4, local copies, waits for them, and re-layouts, front(): piece = lined[k * span:(k + 1) * span]  3.75 us
    ppermute x6, starting transfers between devices, front(): halos.append((lax.ppermute(tail, 'tm', up), lax.ppermute(head, 'tm', down)))  3.55 us
    slice x3, local copies, waits for them, and re-layouts, front(): tail, head = (piece[:, :, own - hist:], piece[:, :, :hist])  2.81 us
  transfers between devices with their start and end apart: 6, of which 3 were waited for; matrix products, arithmetic and copies ran while one was open for 4% of the time, Pallas kernels for 10%

profile of v5, /device:TPU:11, one launch (start us, length us, event | category | flops | bytes accessed | tf_op | source)
XLA Modules:
  0.0 131.9 jit_solution(7684564027397104817)
XLA Ops:
  0.0 2.6 %fusion = (bf16[24,2,6144]{2,1,0:T(2,128)(2,1)S(1)}, bf16[24,2,6144]{2,1,0:T(2,128)(2,1)S(1)}, bf16[24,2,6144]{2,1,0:T(2,128)(2,1)S(1)}) fusion(bf16[72,2,6144]{2,1,0:T(2,128)(2,1)} %param.5), kind=kLoop, calls=%fused_computation.1 | loop fusion | bytes 3538944 | tf_op jit(solution)/shard_map/slice | solution.py:131
  2.6 0.4 slice.45
  3.0 1.0 fusion.1
  4.0 0.7 collective-permute-start.5
  4.7 1.1 collective-permute-start.4
  5.8 0.4 slice.41
  6.2 1.0 fusion.2
  7.2 0.0 collective-permute-start.3
  7.2 1.7 %collective-permute-start.2 = (bf16[24,2,32,128]{3,2,1,0:T(8,128)(2,1)}, bf16[24,2,32,128]{3,2,1,0:T(8,128)(2,1)}, u32[]{:S(2)}, u32[]{:S(2)}) collective-permute-start(bf16[24,2,32,128]{3,2,1,0:T(8,128)(2,1)} %get-tuple-element.11), channel_id=1, source_target_pairs={{0,1},{1,2},{2,3},{3,0},{4,5},{5,6},{6,7},{7,4},{8,9},{9,10},{10,1... | collective-permute-start | bytes 1179656 | tf_op jit(solution)/shard_map/ppermute | solution.py:133
  8.9 0.4 slice.37
  9.3 0.9 fusion.3
  10.1 2.4 %reshape.12.own_ref = bf16[72,2,48,128]{3,2,1,0:T(8,128)(2,1)} reshape(bf16[72,2,6144]{2,1,0:T(2,128)(2,1)S(1)} %copy-done) | data formatting | bytes 3538944 | tf_op jit(solution)/shard_map/reshape | solution.py:128
  12.5 2.7 %collective-permute-done.5.after_ref = bf16[24,2,32,128]{3,2,1,0:T(8,128)(2,1)} collective-permute-done((bf16[24,2,32,128]{3,2,1,0:T(8,128)(2,1)}, bf16[24,2,32,128]{3,2,1,0:T(8,128)(2,1)}, u32[]{:S(2)}, u32[]{:S(2)}) %collective-permute-start.5) | collective-permute-done | bytes 393248 | tf_op jit(solution)/shard_map/ppermute | solution.py:133
  15.2 0.7 broadcast_in_dim.8.coef_ref
  15.9 6.8 %spectra.3.rest_0_ = bf16[8,9,96,128]{3,2,1,0:T(8,128)(2,1)} custom-call(s32[72]{0:T(128)} %delays_ref.5, bf16[24,2,32,128]{3,2,1,0:T(8,128)(2,1)} %collective-permute-done.4.before_ref, bf16[72,2,48,128]{3,2,1,0:T(8,128)(2,1)} %reshape.12.own_ref, bf16[24,2,32,128]{3,2,1,0:T(8,128)(2,1)} %collective-permute-done.5.after_ref, ...), custom_call_target="tpu_custom_call" | custom-call | flops 905969664 | bytes 16777216 | tf_op jit(solution)/shard_map/spectra/pallas_call | solution.py:163
  22.7 0.9 collective-permute-done.3.after_ref
  23.6 0.8 copy-done.1
  24.4 6.8 %spectra.4.rest_0_ = bf16[8,9,96,128]{3,2,1,0:T(8,128)(2,1)} custom-call(s32[72]{0:T(128)} %delays_ref.5, bf16[24,2,32,128]{3,2,1,0:T(8,128)(2,1)} %collective-permute-done.2.before_ref, bf16[72,2,48,128]{3,2,1,0:T(8,128)(2,1)} %reshape.12.own_ref, bf16[24,2,32,128]{3,2,1,0:T(8,128)(2,1)} %copy-done.1, ...), custom_call_target="tpu_custom_call", output_to_operand_aliasing={{}: (7, {})} | custom-call | flops 905969664 | bytes 16777216 | tf_op jit(solution)/shard_map/spectra/pallas_call | solution.py:163
  31.2 0.7 collective-permute-done.1.after_ref
  31.9 0.8 copy-done.2
  32.7 0.7 copy-done.3
  33.4 6.9 %spectra.5.sent_ref = bf16[8,9,96,128]{3,2,1,0:T(8,128)(2,1)} custom-call(s32[72]{0:T(128)} %delays_ref.5, bf16[24,2,32,128]{3,2,1,0:T(8,128)(2,1)} %copy-done.3, bf16[72,2,48,128]{3,2,1,0:T(8,128)(2,1)} %reshape.12.own_ref, bf16[24,2,32,128]{3,2,1,0:T(8,128)(2,1)} %copy-done.2, ...), custom_call_target="tpu_custom_call", output_to_operand_aliasing={{}: (7, {})} | custom-call | flops 905969664 | bytes 16777216 | tf_op jit(solution)/shard_map/spectra/pallas_call | solution.py:163
  40.3 60.9 %exchange.1.buf_ref = bf16[4,8,9,96,128]{4,3,2,1,0:T(8,128)(2,1)} custom-call(bf16[8,9,96,128]{3,2,1,0:T(8,128)(2,1)} %spectra.5.sent_ref), custom_call_target="tpu_custom_call" | custom-call | tf_op jit(solution)/shard_map/exchange/pallas_call | solution.py:305
  101.2 30.7 %turned_gram.1 = f32[32,144,1152]{2,1,0:T(8,128)} custom-call(s32[1]{0:T(128)} %bitcast.which_ref, bf16[4,8,9,96,128]{4,3,2,1,0:T(8,128)(2,1)} %exchange.1.buf_ref), custom_call_target="tpu_custom_call" | custom-call | tf_op jit(solution)/shard_map/turned_gram/pallas_call | solution.py:387
  (14 shorter events, 0.0 us)
Async XLA Ops:
  4.0 11.2 %collective-permute-start.5 = (bf16[24,2,32,128]{3,2,1,0:T(8,128)(2,1)}, bf16[24,2,32,128]{3,2,1,0:T(8,128)(2,1)}, u32[]{:S(2)}, u32[]{:S(2)}) collective-permute-start(bf16[24,2,32,128]{3,2,1,0:T(8,128)(2,1)} %get-tuple-element.8), channel_id=1, source_target_pairs={{1,0},{2,1},{3,2},{0,3},{5,4},{6,5},{7,6},{4,7},{9,8},{10,9},{11,1... | collective-permute-start | bytes 1179656 | tf_op jit(solution)/shard_map/ppermute | solution.py:133
  4.7 10.6 %collective-permute-start.4 = (bf16[24,2,32,128]{3,2,1,0:T(8,128)(2,1)}, bf16[24,2,32,128]{3,2,1,0:T(8,128)(2,1)}, u32[]{:S(2)}, u32[]{:S(2)}) collective-permute-start(bf16[24,2,32,128]{3,2,1,0:T(8,128)(2,1)} %get-tuple-element.9), channel_id=1, source_target_pairs={{0,1},{1,2},{2,3},{3,0},{4,5},{5,6},{6,7},{7,4},{8,9},{9,10},{10,1... | collective-permute-start | bytes 1179656 | tf_op jit(solution)/shard_map/ppermute | solution.py:133
  7.2 3.0 %copy-start = (bf16[72,2,6144]{2,1,0:T(2,128)(2,1)S(1)}, bf16[72,2,6144]{2,1,0:T(2,128)(2,1)}, u32[]{:S(2)}) copy-start(bf16[72,2,6144]{2,1,0:T(2,128)(2,1)} %param.5) | copy-start | bytes 5308420
  7.2 16.5 %collective-permute-start.3 = (bf16[24,2,32,128]{3,2,1,0:T(8,128)(2,1)}, bf16[24,2,32,128]{3,2,1,0:T(8,128)(2,1)S(1)}, u32[]{:S(2)}, u32[]{:S(2)}) collective-permute-start(bf16[24,2,32,128]{3,2,1,0:T(8,128)(2,1)} %get-tuple-element.10), channel_id=1, source_target_pairs={{1,0},{2,1},{3,2},{0,3},{5,4},{6,5},{7,6},{4,7},{9,8},{10,9},{11,1... | collective-permute-start | bytes 1179656 | tf_op jit(solution)/shard_map/ppermute | solution.py:133
  7.2 16.5 %collective-permute-start.2 = (bf16[24,2,32,128]{3,2,1,0:T(8,128)(2,1)}, bf16[24,2,32,128]{3,2,1,0:T(8,128)(2,1)}, u32[]{:S(2)}, u32[]{:S(2)}) collective-permute-start(bf16[24,2,32,128]{3,2,1,0:T(8,128)(2,1)} %get-tuple-element.11), channel_id=1, source_target_pairs={{0,1},{1,2},{2,3},{3,0},{4,5},{5,6},{6,7},{7,4},{8,9},{9,10},{10,1... | collective-permute-start | bytes 1179656 | tf_op jit(solution)/shard_map/ppermute | solution.py:133
  10.1 21.8 %collective-permute-start.1 = (bf16[24,2,32,128]{3,2,1,0:T(8,128)(2,1)}, bf16[24,2,32,128]{3,2,1,0:T(8,128)(2,1)S(1)}, u32[]{:S(2)}, u32[]{:S(2)}) collective-permute-start(bf16[24,2,32,128]{3,2,1,0:T(8,128)(2,1)} %get-tuple-element.12), channel_id=1, source_target_pairs={{1,0},{2,1},{3,2},{0,3},{5,4},{6,5},{7,6},{4,7},{9,8},{10,9},{11,1... | collective-permute-start | bytes 1179656 | tf_op jit(solution)/shard_map/ppermute | solution.py:133
  10.1 5.1 %copy-start.4 = (s32[16,256]{1,0:T(8,128)S(1)}, s32[16,256]{1,0:T(8,128)}, u32[]{:S(2)}) copy-start(s32[16,256]{1,0:T(8,128)} %param.7) | copy-start | bytes 49156
  15.2 16.8 %collective-permute-start = (bf16[24,2,32,128]{3,2,1,0:T(8,128)(2,1)S(1)}, bf16[24,2,32,128]{3,2,1,0:T(8,128)(2,1)S(1)}, u32[]{:S(2)}, u32[]{:S(2)}) collective-permute-start(bf16[24,2,32,128]{3,2,1,0:T(8,128)(2,1)S(1)} %get-tuple-element.13), channel_id=1, source_target_pairs={{0,1},{1,2},{2,3},{3,0},{4,5},{5,6},{6,7},{7,4},{8,9},{9,10},{10,1... | collective-permute-start | bytes 1179656 | tf_op jit(solution)/shard_map/ppermute | solution.py:133
  23.6 0.8 copy-start.1
  31.9 0.8 copy-start.2
  32.7 0.7 copy-start.3
